TPU v7x, 256 devices: a whole 4x4x8 slice. The times are simulated.
256 devices in a mesh: nodes: 64 (over z, x, core), fsdp: 4 (over y).
Axes of the slice: x: 4, y: 4, z: 8, core: 2. Of those that a mesh axis runs over, the one named last changes fastest.
Arguments:
- features: bfloat16 [512, 4, 128, 1024], P('nodes', 'fsdp'), may hold values from -6 to 6
- norm_gain: float32 [1024], replicated, may hold values from 0.25 to 1.75
- query_weight: bfloat16 [1024, 1024], P('fsdp'), may hold values from -1 to 1
- key_weight: bfloat16 [1024, 1024], P('fsdp'), may hold values from -1 to 1
- value_weight: bfloat16 [1024, 1024], P('fsdp'), may hold values from -0.1875 to 0.1875
- output_weight: bfloat16 [1024, 1024], P('fsdp'), may hold values from -0.1875 to 0.1875
- adjacency: int32 [512, 4, 8], P('nodes', 'fsdp'), may hold values from 0 to 511, as said below
- valid: int32 [512, 4, 8], P('nodes', 'fsdp'), may hold values 0 or 1
Outputs:
- updated: bfloat16 [512, 4, 128, 1024], P('nodes', 'fsdp')
Inputs may be any that keep to these rules, and one draw needn't show every extreme that they name: adjacency[r, c, j] differs from r by 1 to 8; slots may repeat a cluster.
All inputs are finite; a program needn't handle non-finite values. No bound on the sum of `valid` on one device may be relied on, other than what follows from the above.
Results may differ from a plain program's by a relative error of at most 0.0047.
Values may be sent and summed in bfloat16 or wider, within the bound.
No kernel may reach another device: no remote copies, remote signals or barrier semaphores. Data moves between devices by JAX's collectives and lax.ppermute only.
A program may use at most 128 MiB of HBM per device.

v0:
```python
import jax
import jax.numpy as jnp
from jax import lax
from jax.sharding import PartitionSpec as P

HEADS = 16
HSIZE = 64


def extended(cells, sides, width):
    for axis, dim in sides:
        count = lax.axis_size(axis)
        ends = count - 1
        head = lax.slice_in_dim(cells, 0, width, axis=dim)
        tail = lax.slice_in_dim(cells, cells.shape[dim] - width, cells.shape[dim], axis=dim)
        cells = jnp.concatenate(
            [
                lax.ppermute(tail, axis, [(i, (i + 1) % count) for i in range(ends)]),
                cells,
                lax.ppermute(head, axis, [((i + 1) % count, i) for i in range(ends)]),
            ],
            axis=dim,
        )
    return cells


def attend(queries, key_rows, key_keep):
    count = queries.shape[0]
    model_width = queries.shape[1]
    query_heads = queries.reshape(count, HEADS, HSIZE)
    key_heads = key_rows[:, :model_width].reshape(-1, HEADS, HSIZE)
    value_heads = key_rows[:, model_width:].reshape(-1, HEADS, HSIZE)
    scores = jnp.einsum(
        "qhd,khd->hqk", query_heads, key_heads, preferred_element_type=jnp.float32
    ) * (1.0 / HSIZE**0.5)
    scores = jnp.where(key_keep[None, None, :] > 0, scores, -1e30)
    largest = jnp.max(scores, axis=-1, keepdims=True)
    weights_exp = jnp.exp(scores - largest)
    denominator = jnp.sum(weights_exp, axis=-1, keepdims=True)
    probs = (weights_exp / denominator).astype(jnp.bfloat16)
    context = jnp.einsum("hqk,khd->qhd", probs, value_heads, preferred_element_type=jnp.float32)
    return context.reshape(count, model_width).astype(jnp.bfloat16)


def add_columns(left, piece):
    return jnp.dot(left, piece, preferred_element_type=jnp.float32)


def per_device(
    features, norm_gain, query_weight, key_weight, value_weight, output_weight, adjacency, valid
):
    cluster_rows = features.shape[0]
    cluster_size = features.shape[2]
    model_width = features.shape[3]
    node_rows = cluster_rows * cluster_size
    wide = features.reshape(node_rows, model_width).astype(jnp.float32)
    mean_square = jnp.mean(wide * wide, axis=-1, keepdims=True)
    normed = (wide * lax.rsqrt(mean_square + 1e-06) * norm_gain[None, :]).astype(jnp.bfloat16)
    query_sum = add_columns(normed, lax.all_gather(query_weight, "fsdp", axis=0, tiled=True))
    key_sum = add_columns(normed, lax.all_gather(key_weight, "fsdp", axis=0, tiled=True))
    value_sum = add_columns(normed, lax.all_gather(value_weight, "fsdp", axis=0, tiled=True))
    queries = query_sum.astype(jnp.bfloat16)
    key_value = jnp.concatenate(
        [key_sum.astype(jnp.bfloat16), value_sum.astype(jnp.bfloat16)], axis=-1
    )
    key_value = key_value.reshape(cluster_rows, 1, cluster_size, 2 * model_width)
    window = extended(key_value, (("nodes", 0),), cluster_rows)
    window = window.reshape(3 * cluster_rows, cluster_size, 2 * model_width)
    first_row = lax.axis_index("nodes") * cluster_rows
    local_index = adjacency[:, 0, :] - first_row + cluster_rows
    query_blocks = queries.reshape(cluster_rows, cluster_size, model_width)

    def one_cluster(packed):
        position, query_block, neighbor_rows, neighbor_valid = packed
        own = lax.dynamic_index_in_dim(window, position + cluster_rows, 0, keepdims=True)
        others = jnp.take(window, neighbor_rows, axis=0)
        key_rows = jnp.concatenate([own, others], axis=0).reshape(-1, 2 * model_width)
        slot_keep = jnp.concatenate([jnp.ones((1,), jnp.int32), neighbor_valid])
        key_keep = jnp.repeat(slot_keep, cluster_size)
        return attend(query_block, key_rows, key_keep)

    context = lax.map(
        one_cluster,
        (jnp.arange(cluster_rows, dtype=jnp.int32), query_blocks, local_index, valid[:, 0, :]),
    )
    context = context.reshape(node_rows, model_width)
    projected = add_columns(context, lax.all_gather(output_weight, "fsdp", axis=0, tiled=True))
    updated = (wide + projected).astype(jnp.bfloat16)
    return updated.reshape(cluster_rows, 1, cluster_size, model_width)


def solution(mesh):
    in_specs = (
        P("nodes", "fsdp", None, None),
        P(),
        P("fsdp", None),
        P("fsdp", None),
        P("fsdp", None),
        P("fsdp", None),
        P("nodes", "fsdp", None),
        P("nodes", "fsdp", None),
    )
    out_specs = P("nodes", "fsdp", None, None)
    return jax.shard_map(
        per_device, mesh=mesh, in_specs=in_specs, out_specs=out_specs, check_vma=False
    )
```

profile of v0, /device:TPU:103, one launch (start us, length us, event | category | flops | bytes accessed | tf_op | source)
XLA Modules:
  0.0 492.6 jit_solution(7598226909542608656)
XLA Ops:
  12.0 32.4 %all-gather.7.cloned.1.call-done = bf16[1024,1024]{1,0:T(8,128)(2,1)} async-done(((bf16[256,1024]{1,0:T(8,128)(2,1)}), bf16[1024,1024]{1,0:T(8,128)(2,1)}) %all-gather.7.cloned.1.call-update) | async-done | bytes 2097168 | tf_op jit(solution)/shard_map/all_gather | solution.py:61
  50.4 29.3 %all-gather.5.cloned.1.call-done = bf16[1024,1024]{1,0:T(8,128)(2,1)} async-done(((bf16[256,1024]{1,0:T(8,128)(2,1)}), bf16[1024,1024]{1,0:T(8,128)(2,1)}) %all-gather.5.cloned.1.call-update) | async-done | bytes 2097168 | tf_op jit(solution)/shard_map/all_gather | solution.py:60
  86.3 6.5 %copy.21 = bf16[1024,2048]{1,0:T(8,128)(2,1)} copy(bf16[1024,2048]{0,1:T(8,128)(2,1)} %pad_maximum_fusion.1) | data formatting | bytes 8388608 | tf_op jit(solution)/shard_map/reshape | solution.py:66
  100.3 32.6 %all-gather.9.cloned.1.call-done = bf16[1024,1024]{1,0:T(8,128)(2,1)} async-done(((bf16[256,1024]{1,0:T(8,128)(2,1)}), bf16[1024,1024]{1,0:T(8,128)(2,1)}) %all-gather.9.cloned.1.call-update) | async-done | bytes 2097168 | tf_op jit(solution)/shard_map/all_gather | solution.py:59
  143.5 7.7 %collective-permute-done.1 = bf16[8,1,128,2048]{3,2,0,1:T(8,128)(2,1)} collective-permute-done((bf16[8,1,128,2048]{3,2,0,1:T(8,128)(2,1)}, bf16[8,1,128,2048]{3,2,0,1:T(8,128)(2,1)}, u32[]{:S(2)}, u32[]{:S(2)}) %collective-permute-start.1) | collective-permute-done | bytes 4194336 | tf_op jit(solution)/shard_map/ppermute | solution.py:20
  151.2 9.9 %maximum_bitcast_fusion = bf16[24,128,2048]{2,1,0:T(8,128)(2,1)} fusion(bf16[8,1,128,2048]{3,2,0,1:T(8,128)(2,1)} %collective-permute-done.1, bf16[8,1,128,2048]{3,2,0,1:T(8,128)(2,1)S(1)} %bitcast.88, bf16[8,1,128,2048]{3,2,0,1:T(8,128)(2,1)} %collective-permute-done), kind=kLoop, calls=%fused_computation.29 | loop fusion | flops 12582912 | bytes 25165824 | tf_op jit(solution)/shard_map/reshape | solution.py:68
  161.1 318.5 %while.12 = (s32[]{:T(128)}, bf16[8,128,1024]{2,1,0:T(8,128)(2,1)}, s32[8]{0:T(128)S(1)}, bf16[24,128,2048]{2,1,0:T(8,128)(2,1)}, s32[8,8]{1,0:T(8,128)S(1)}, /*...) while((s32[]{:T(128)}, bf16[8,128,1024]{2,1,0:T(8,128)(2,1)}, ...), condition=%wide.region_4.5_spmd, body=%wide.region_1.4_spmd.sunk | while | flops 622725376 | bytes 72375528 | solution.py:82
  164.3 7.3 %gather_fusion = bf16[8,128,2048]{2,1,0:T(8,128)(2,1)} fusion(bf16[24,128,2048]{2,1,0:T(8,128)(2,1)} %get-tuple-element.205, s32[1024]{0:T(1024)S(1)} %pad_clamp_fusion.2), kind=kCustom, calls=%fused_computation.clone.1 | custom fusion | bytes 8388640 | tf_op jit(solution)/shard_map/while/body/eval_jaxpr/jit(_take)/gather | solution.py:76
  183.0 8.2 %fusion.44 = (f32[16,128]{1,0:T(8,128)S(1)}, f32[16,128,1152]{2,1,0:T(8,128)}) fusion(pred[1152]{0:T(1024)(128)(4,1)S(1)} %broadcast_bitcast_fusion.2, bf16[128,16,64]{0,2,1:T(8,128)(2,1)S(1)} %bitcast.89, bf16[1152,16,64]{0,2,1:T(8,128)(2,1)} %bitcast.84), kind=kOutput, calls=%fused_computation.44.clone.1 | convolution fusion | flops 311428224 | bytes 12067968 | tf_op jit(solution)/shard_map/while/body/eval_jaxpr/sub | solution.py:38
  204.1 7.3 %gather_fusion = bf16[8,128,2048]{2,1,0:T(8,128)(2,1)} fusion(bf16[24,128,2048]{2,1,0:T(8,128)(2,1)} %get-tuple-element.205, s32[1024]{0:T(1024)S(1)} %pad_clamp_fusion.2), kind=kCustom, calls=%fused_computation.clone.1 | custom fusion | bytes 8388640 | tf_op jit(solution)/shard_map/while/body/eval_jaxpr/jit(_take)/gather | solution.py:76
  222.8 8.2 %fusion.44 = (f32[16,128]{1,0:T(8,128)S(1)}, f32[16,128,1152]{2,1,0:T(8,128)}) fusion(pred[1152]{0:T(1024)(128)(4,1)S(1)} %broadcast_bitcast_fusion.2, bf16[128,16,64]{0,2,1:T(8,128)(2,1)S(1)} %bitcast.89, bf16[1152,16,64]{0,2,1:T(8,128)(2,1)} %bitcast.84), kind=kOutput, calls=%fused_computation.44.clone.1 | convolution fusion | flops 311428224 | bytes 12067968 | tf_op jit(solution)/shard_map/while/body/eval_jaxpr/sub | solution.py:38
  243.9 7.3 %gather_fusion = bf16[8,128,2048]{2,1,0:T(8,128)(2,1)} fusion(bf16[24,128,2048]{2,1,0:T(8,128)(2,1)} %get-tuple-element.205, s32[1024]{0:T(1024)S(1)} %pad_clamp_fusion.2), kind=kCustom, calls=%fused_computation.clone.1 | custom fusion | bytes 8388640 | tf_op jit(solution)/shard_map/while/body/eval_jaxpr/jit(_take)/gather | solution.py:76
  262.6 8.2 %fusion.44 = (f32[16,128]{1,0:T(8,128)S(1)}, f32[16,128,1152]{2,1,0:T(8,128)}) fusion(pred[1152]{0:T(1024)(128)(4,1)S(1)} %broadcast_bitcast_fusion.2, bf16[128,16,64]{0,2,1:T(8,128)(2,1)S(1)} %bitcast.89, bf16[1152,16,64]{0,2,1:T(8,128)(2,1)} %bitcast.84), kind=kOutput, calls=%fused_computation.44.clone.1 | convolution fusion | flops 311428224 | bytes 12067968 | tf_op jit(solution)/shard_map/while/body/eval_jaxpr/sub | solution.py:38
  283.8 7.3 %gather_fusion = bf16[8,128,2048]{2,1,0:T(8,128)(2,1)} fusion(bf16[24,128,2048]{2,1,0:T(8,128)(2,1)} %get-tuple-element.205, s32[1024]{0:T(1024)S(1)} %pad_clamp_fusion.2), kind=kCustom, calls=%fused_computation.clone.1 | custom fusion | bytes 8388640 | tf_op jit(solution)/shard_map/while/body/eval_jaxpr/jit(_take)/gather | solution.py:76
  302.5 8.2 %fusion.44 = (f32[16,128]{1,0:T(8,128)S(1)}, f32[16,128,1152]{2,1,0:T(8,128)}) fusion(pred[1152]{0:T(1024)(128)(4,1)S(1)} %broadcast_bitcast_fusion.2, bf16[128,16,64]{0,2,1:T(8,128)(2,1)S(1)} %bitcast.89, bf16[1152,16,64]{0,2,1:T(8,128)(2,1)} %bitcast.84), kind=kOutput, calls=%fused_computation.44.clone.1 | convolution fusion | flops 311428224 | bytes 12067968 | tf_op jit(solution)/shard_map/while/body/eval_jaxpr/sub | solution.py:38
  323.6 7.3 %gather_fusion = bf16[8,128,2048]{2,1,0:T(8,128)(2,1)} fusion(bf16[24,128,2048]{2,1,0:T(8,128)(2,1)} %get-tuple-element.205, s32[1024]{0:T(1024)S(1)} %pad_clamp_fusion.2), kind=kCustom, calls=%fused_computation.clone.1 | custom fusion | bytes 8388640 | tf_op jit(solution)/shard_map/while/body/eval_jaxpr/jit(_take)/gather | solution.py:76
  342.3 8.2 %fusion.44 = (f32[16,128]{1,0:T(8,128)S(1)}, f32[16,128,1152]{2,1,0:T(8,128)}) fusion(pred[1152]{0:T(1024)(128)(4,1)S(1)} %broadcast_bitcast_fusion.2, bf16[128,16,64]{0,2,1:T(8,128)(2,1)S(1)} %bitcast.89, bf16[1152,16,64]{0,2,1:T(8,128)(2,1)} %bitcast.84), kind=kOutput, calls=%fused_computation.44.clone.1 | convolution fusion | flops 311428224 | bytes 12067968 | tf_op jit(solution)/shard_map/while/body/eval_jaxpr/sub | solution.py:38
  363.4 7.3 %gather_fusion = bf16[8,128,2048]{2,1,0:T(8,128)(2,1)} fusion(bf16[24,128,2048]{2,1,0:T(8,128)(2,1)} %get-tuple-element.205, s32[1024]{0:T(1024)S(1)} %pad_clamp_fusion.2), kind=kCustom, calls=%fused_computation.clone.1 | custom fusion | bytes 8388640 | tf_op jit(solution)/shard_map/while/body/eval_jaxpr/jit(_take)/gather | solution.py:76
  382.1 8.2 %fusion.44 = (f32[16,128]{1,0:T(8,128)S(1)}, f32[16,128,1152]{2,1,0:T(8,128)}) fusion(pred[1152]{0:T(1024)(128)(4,1)S(1)} %broadcast_bitcast_fusion.2, bf16[128,16,64]{0,2,1:T(8,128)(2,1)S(1)} %bitcast.89, bf16[1152,16,64]{0,2,1:T(8,128)(2,1)} %bitcast.84), kind=kOutput, calls=%fused_computation.44.clone.1 | convolution fusion | flops 311428224 | bytes 12067968 | tf_op jit(solution)/shard_map/while/body/eval_jaxpr/sub | solution.py:38
  403.2 7.3 %gather_fusion = bf16[8,128,2048]{2,1,0:T(8,128)(2,1)} fusion(bf16[24,128,2048]{2,1,0:T(8,128)(2,1)} %get-tuple-element.205, s32[1024]{0:T(1024)S(1)} %pad_clamp_fusion.2), kind=kCustom, calls=%fused_computation.clone.1 | custom fusion | bytes 8388640 | tf_op jit(solution)/shard_map/while/body/eval_jaxpr/jit(_take)/gather | solution.py:76
  421.9 8.2 %fusion.44 = (f32[16,128]{1,0:T(8,128)S(1)}, f32[16,128,1152]{2,1,0:T(8,128)}) fusion(pred[1152]{0:T(1024)(128)(4,1)S(1)} %broadcast_bitcast_fusion.2, bf16[128,16,64]{0,2,1:T(8,128)(2,1)S(1)} %bitcast.89, bf16[1152,16,64]{0,2,1:T(8,128)(2,1)} %bitcast.84), kind=kOutput, calls=%fused_computation.44.clone.1 | convolution fusion | flops 311428224 | bytes 12067968 | tf_op jit(solution)/shard_map/while/body/eval_jaxpr/sub | solution.py:38
  443.0 7.3 %gather_fusion = bf16[8,128,2048]{2,1,0:T(8,128)(2,1)} fusion(bf16[24,128,2048]{2,1,0:T(8,128)(2,1)} %get-tuple-element.205, s32[1024]{0:T(1024)S(1)} %pad_clamp_fusion.2), kind=kCustom, calls=%fused_computation.clone.1 | custom fusion | bytes 8388640 | tf_op jit(solution)/shard_map/while/body/eval_jaxpr/jit(_take)/gather | solution.py:76
  461.7 8.2 %fusion.44 = (f32[16,128]{1,0:T(8,128)S(1)}, f32[16,128,1152]{2,1,0:T(8,128)}) fusion(pred[1152]{0:T(1024)(128)(4,1)S(1)} %broadcast_bitcast_fusion.2, bf16[128,16,64]{0,2,1:T(8,128)(2,1)S(1)} %bitcast.89, bf16[1152,16,64]{0,2,1:T(8,128)(2,1)} %bitcast.84), kind=kOutput, calls=%fused_computation.44.clone.1 | convolution fusion | flops 311428224 | bytes 12067968 | tf_op jit(solution)/shard_map/while/body/eval_jaxpr/sub | solution.py:38
  479.6 6.5 %fusion.16 = bf16[1024,1024]{1,0:T(8,128)(2,1)} fusion(bf16[8,1,128,1024]{3,2,1,0:T(8,128)(2,1)} %param.10, bf16[1024,1024]{1,0:T(8,128)(2,1)} %bitcast.93, bf16[1024,1024]{1,0:T(8,128)(2,1)} %all-gather.11.cloned.1.call-done), kind=kOutput, calls=%fused_computation.37 | convolution fusion | flops 2150629376 | bytes 8388608 | tf_op jit(solution)/shard_map/dot_general | solution.py:46
  (178 shorter events, 218.9 us)
Async XLA Ops:
  6.5 3.6 copy-start.1
  6.5 3.6 copy-start.5
  6.5 37.9 %all-gather.7.cloned.1.call-start = ((), (), s32[]{:S(2)}) async-start(), calls=%async_computation.1 | async-start | bytes 2621440 | tf_op jit(solution)/shard_map/all_gather | solution.py:61
  7.3 72.5 %all-gather.5.cloned.1.call-start = ((), (), s32[]{:S(2)}) async-start(), calls=%async_computation | async-start | bytes 2621440 | tf_op jit(solution)/shard_map/all_gather | solution.py:60
  8.0 124.9 %all-gather.9.cloned.1.call-start = ((), (), s32[]{:S(2)}) async-start(), calls=%async_computation.2 | async-start | bytes 2621440 | tf_op jit(solution)/shard_map/all_gather | solution.py:59
  12.0 67.7 %copy-start.2 = (bf16[1024,1024]{1,0:T(8,128)(2,1)S(1)}, bf16[1024,1024]{1,0:T(8,128)(2,1)}, u32[]{:S(2)}) copy-start(bf16[1024,1024]{1,0:T(8,128)(2,1)} %fusion.15) | copy-start | bytes 6291460
  79.7 4.1 copy-start.3
  86.3 14.0 %copy-start.4 = (s32[8,1,8]{2,1,0:T(1,128)S(1)}, s32[8,1,8]{2,1,0:T(1,128)}, u32[]{:S(2)}) copy-start(s32[8,1,8]{2,1,0:T(1,128)} %param.16) | copy-start | bytes 772
  92.8 50.7 %collective-permute-start = (bf16[8,1,128,2048]{3,2,0,1:T(8,128)(2,1)}, bf16[8,1,128,2048]{3,2,0,1:T(8,128)(2,1)}, u32[]{:S(2)}, u32[]{:S(2)}) collective-permute-start(bf16[8,1,128,2048]{3,2,0,1:T(8,128)(2,1)} %bitcast.86), channel_id=1, source_target_pairs={{0,4},{4,8},{8,12},{12,16},{16,20},{20,24},{24,28},{28,32},{32,36}... | collective-permute-start | bytes 12582920 | tf_op jit(solution)/shard_map/ppermute | solution.py:18
  97.8 53.5 %collective-permute-start.1 = (bf16[8,1,128,2048]{3,2,0,1:T(8,128)(2,1)}, bf16[8,1,128,2048]{3,2,0,1:T(8,128)(2,1)}, u32[]{:S(2)}, u32[]{:S(2)}) collective-permute-start(bf16[8,1,128,2048]{3,2,0,1:T(8,128)(2,1)} %bitcast.87), channel_id=1, source_target_pairs={{4,0},{8,4},{12,8},{16,12},{20,16},{24,20},{28,24},{32,28},{36,32}... | collective-permute-start | bytes 12582920 | tf_op jit(solution)/shard_map/ppermute | solution.py:20
  99.7 379.9 %all-gather.11.cloned.1.call-start = ((), (), s32[]{:S(2)}) async-start(), calls=%async_computation.3 | async-start | bytes 2621440 | tf_op jit(solution)/shard_map/all_gather | solution.py:87
  132.9 18.3 %copy-start = (bf16[1024,2048]{1,0:T(8,128)(2,1)S(1)}, bf16[1024,2048]{1,0:T(8,128)(2,1)}, u32[]{:S(2)}) copy-start(bf16[1024,2048]{1,0:T(8,128)(2,1)} %copy.21) | copy-start | bytes 12582916
Sparse Core Ops, SparseCore 0:
  9.2 35.2 all-gather.6
  46.2 33.4 all-gather.4
  99.8 33.0 all-gather.8
  134.6 33.4 all-gather.10
where the time goes:
time: 496 us; the launch traced here: 493 us
  local copies, waits for them, and re-layouts  172 us (35%)
  matrix products  138 us (28%)
  waiting for transfers between devices  109 us (22%)
  other arithmetic  41.6 us (8%)
  between operations  13.2 us (3%)
  loops' own time  11.6 us (2%)
  starting transfers between devices  7.15 us (1%)
    sub x8, matrix products, attend(): weights_exp = jnp.exp(scores - largest)  65.3 us
    gather x8, local copies, waits for them, and re-layouts, one_cluster(): others = jnp.take(window, neighbor_rows, axis=0)  58.5 us
    dot_general x8, matrix products, attend(): jnp.einsum('hqk,khd->qhd', probs, value_heads, preferred_element_type=jnp...  51 us
    slice x16, local copies, waits for them, and re-layouts, attend(): key_heads = key_rows[:, :model_width].reshape(-1, HEADS, HSIZE)  50.4 us
    all_gather x1, waiting for transfers between devices, per_device(): lax.all_gather(query_weight, 'fsdp', axis=0, tiled=True)  32.6 us
    all_gather x1, waiting for transfers between devices, per_device(): lax.all_gather(value_weight, 'fsdp', axis=0, tiled=True)  32.4 us
    all_gather x1, waiting for transfers between devices, per_device(): lax.all_gather(key_weight, 'fsdp', axis=0, tiled=True)  29.3 us
    dot_general x4, matrix products, add_columns(): return jnp.dot(left, piece, preferred_element_type=jnp.float32)  22 us
  transfers between devices with their start and end apart: 6, of which 5 were waited for; matrix products, arithmetic and copies ran while one was open for 67% of the time, Pallas kernels for 0%

commit v1 on v0

v1 whole, which is shorter than its diff:
```python
import functools

import jax
import jax.numpy as jnp
from jax import lax
from jax.experimental import pallas as pl
from jax.experimental.pallas import tpu as pltpu
from jax.sharding import Mesh
from jax.sharding import PartitionSpec as P

BF = jnp.bfloat16
F32 = jnp.float32
NODES = ("z", "x", "core")
HSIZE = 64
QSCALE = 1.4426950408889634 / HSIZE**0.5
ROWS = 8
CS = 128
D = 1024
TILE = 256
SHARD = 256


def swap_cores(t):
    return lax.ppermute(t, "core", [(0, 1), (1, 0)])


def gather_pieces(shards):
    up = [(i, (i + 1) % 4) for i in range(4)]
    down = [((i + 1) % 4, i) for i in range(4)]
    half = shards.shape[0] // 2
    a = lax.ppermute(shards, "fsdp", up)
    b = lax.ppermute(shards, "fsdp", down)
    c = lax.ppermute(a[:half], "fsdp", up)
    d = lax.ppermute(b[half:], "fsdp", down)
    return (a, b, c, d), tuple(swap_cores(t) for t in (a, b, c, d))


def half_rows(weight):
    core = lax.axis_index("core")
    return lax.dynamic_slice_in_dim(weight, core * (SHARD // 2), SHARD // 2, 0)


def place_halves(own, mine, other):
    y = lax.axis_index("fsdp")
    core = lax.axis_index("core")
    h = SHARD // 2
    pieces = [own]
    starts = [y * SHARD]
    for part, c in ((mine, core), (other, 1 - core)):
        a, b, e, f = part
        pieces += [a, b, e, f]
        starts += [
            (y + 3) % 4 * SHARD + c * h,
            (y + 1) % 4 * SHARD + c * h,
            (y + 2) % 4 * SHARD + c * h,
            (y + 2) % 4 * SHARD + c * h + h // 2,
        ]
    return pieces, starts


def project_kernel(starts, x_ref, gain_ref, *refs, count, per, scales, aliased):
    pieces = refs[: count * per]
    refs = refs[count * per + (count if aliased else 0) :]
    outs, (weights, sems) = refs[:count], refs[count:]
    step = pl.program_id(0)

    def copies():
        for w in range(count):
            for p in range(per):
                piece = pieces[w * per + p]
                rows = piece.shape[0]
                start = pl.multiple_of(starts[w * per + p], 64)
                yield pltpu.make_async_copy(
                    piece, weights.at[w, pl.ds(start, rows)], sems.at[w * per + p]
                )

    @pl.when(step == 0)
    def _():
        for c in copies():
            c.start()
        for c in copies():
            c.wait()

    wide = x_ref[...].astype(F32)
    mean = jnp.mean(wide * wide, axis=-1, keepdims=True)
    normed = (wide * lax.rsqrt(mean + 1e-06) * gain_ref[...]).astype(BF)
    for w in range(count):
        got = jnp.dot(normed, weights[w], preferred_element_type=F32)
        if scales[w] != 1.0:
            got = got * scales[w]
        outs[w][...] = got.astype(BF)


def project(name, x, gain, weights, scales, total, first, into=None):
    count = len(weights)
    per = len(weights[0][0])
    pieces = [p for w in weights for p in w[0]]
    starts = jnp.stack([jnp.asarray(s, jnp.int32) for w in weights for s in w[1]])
    rows = x.shape[0]
    hbm = pl.BlockSpec(memory_space=pl.ANY)
    extra = list(into) if into is not None else []
    kernel = functools.partial(
        project_kernel, count=count, per=per, scales=scales, aliased=bool(extra)
    )
    return pl.pallas_call(
        kernel,
        out_shape=[jax.ShapeDtypeStruct((total, D), BF)] * count,
        grid_spec=pltpu.PrefetchScalarGridSpec(
            num_scalar_prefetch=1,
            grid=(rows // TILE,),
            in_specs=[
                pl.BlockSpec((TILE, D), lambda i, s: (i, 0)),
                pl.BlockSpec((1, D), lambda i, s: (0, 0)),
            ]
            + [hbm] * (len(pieces) + len(extra)),
            out_specs=[pl.BlockSpec((TILE, D), lambda i, s: (i + first // TILE, 0))]
            * count,
            scratch_shapes=[
                pltpu.VMEM((count, D, D), BF),
                pltpu.SemaphoreType.DMA((len(pieces),)),
            ],
        ),
        input_output_aliases={3 + len(pieces) + i: i for i in range(len(extra))},
        compiler_params=pltpu.CompilerParams(vmem_limit_bytes=40 << 20),
        cost_estimate=pl.CostEstimate(
            flops=2 * rows * D * D * count,
            bytes_accessed=2 * (rows * D * (1 + count) + count * D * D),
            transcendentals=0,
        ),
        name=name,
    )(starts, x, gain, *pieces, *extra)


def attend_kernel(
    slots, counts, starts, q_ref, k_ref, v_ref, f_ref, *refs, n_pieces
):
    pieces = refs[:n_pieces]
    o_ref, ctx, acc, weight, sems = refs[n_pieces:]
    group = pl.program_id(0)
    last = pl.num_programs(0) - 1

    def copies():
        for p in range(n_pieces):
            start = pl.multiple_of(starts[p], 64)
            yield pltpu.make_async_copy(
                pieces[p], weight.at[pl.ds(start, pieces[p].shape[0])], sems.at[p]
            )

    @pl.when(group == 0)
    def _():
        for c in copies():
            c.start()

    def cluster(r, carry):
        def variant(blocks):
            def run():
                q = q_ref[r]
                head = lax.broadcasted_iota(jnp.int32, (CS, 4 * HSIZE), 1) // HSIZE
                stacked = jnp.concatenate(
                    [jnp.where(head == h, q, jnp.zeros_like(q)) for h in range(4)], 0
                )
                ids = [slots[r, j] for j in range(blocks)]
                scores = []
                for j in range(0, blocks, 2):
                    keys = jnp.concatenate([k_ref[i] for i in ids[j : j + 2]], 0)
                    scores.append(
                        lax.dot_general(
                            stacked,
                            keys,
                            (((1,), (1,)), ((), ())),
                            preferred_element_type=F32,
                        )
                    )
                top = None
                for s in scores:
                    for t in range(0, s.shape[1], 128):
                        part = s[:, t : t + 128]
                        top = part if top is None else jnp.maximum(top, part)
                top = jnp.max(top, axis=1, keepdims=True)
                probs = [jnp.exp2(s - top).astype(BF) for s in scores]
                left = lax.broadcasted_iota(jnp.int32, (CS, 128), 1) < HSIZE
                for t in range(2):
                    lanes = slice(128 * t, 128 * t + 128)
                    total = None
                    for n, j in enumerate(range(0, blocks, 2)):
                        vals = jnp.concatenate(
                            [v_ref[i, :, lanes] for i in ids[j : j + 2]], 0
                        )
                        both = jnp.concatenate([vals, jnp.ones(vals.shape, BF)], 1)
                        d = jnp.dot(
                            probs[n][256 * t : 256 * t + 256],
                            both,
                            preferred_element_type=F32,
                        )
                        total = d if total is None else total + d
                    c = total[:, :128] / total[:, 128:]
                    ctx[r, :, lanes] = jnp.where(left, c[:CS], c[CS:]).astype(BF)

            return run

        lax.switch(counts[r] - 1, [variant(n) for n in range(1, 10)])
        return carry

    lax.fori_loop(0, ROWS, cluster, 0)

    @pl.when(group == 0)
    def _():
        for c in copies():
            c.wait()

    rows = pl.ds(pl.multiple_of(group * 256, 256), 256)
    part = jnp.dot(
        ctx[...].reshape(ROWS * CS, 256), weight[rows], preferred_element_type=F32
    )

    @pl.when(group == 0)
    def _():
        acc[...] = part

    @pl.when(jnp.logical_and(group > 0, group < last))
    def _():
        acc[...] += part

    @pl.when(group == last)
    def _():
        o_ref[...] = (f_ref[...].astype(F32) + acc[...] + part).astype(BF)


def attend(slots, counts, queries, keys, values, features, weight):
    pieces, starts = weight
    starts = jnp.stack([jnp.asarray(s, jnp.int32) for s in starts])
    n = len(pieces)
    return pl.pallas_call(
        functools.partial(attend_kernel, n_pieces=n),
        out_shape=jax.ShapeDtypeStruct((ROWS * CS, D), BF),
        grid_spec=pltpu.PrefetchScalarGridSpec(
            num_scalar_prefetch=3,
            grid=(4,),
            in_specs=[
                pl.BlockSpec((ROWS, CS, 256), lambda g, *_: (0, 0, g)),
                pl.BlockSpec((3 * ROWS, CS, 256), lambda g, *_: (0, 0, g)),
                pl.BlockSpec((3 * ROWS, CS, 256), lambda g, *_: (0, 0, g)),
                pl.BlockSpec((ROWS * CS, D), lambda g, *_: (0, 0)),
            ]
            + [pl.BlockSpec(memory_space=pl.ANY)] * n,
            out_specs=pl.BlockSpec((ROWS * CS, D), lambda g, *_: (0, 0)),
            scratch_shapes=[
                pltpu.VMEM((ROWS, CS, 256), BF),
                pltpu.VMEM((ROWS * CS, D), F32),
                pltpu.VMEM((D, D), BF),
                pltpu.SemaphoreType.DMA((n,)),
            ],
        ),
        compiler_params=pltpu.CompilerParams(vmem_limit_bytes=60 << 20),
        cost_estimate=pl.CostEstimate(
            flops=20 << 30, bytes_accessed=20 << 20, transcendentals=0
        ),
        name="attend",
    )(slots, counts, starts, queries, keys, values, features, *pieces)


def key_slots(adjacency, valid, node):
    index = adjacency[:, 0, :] - node * ROWS + ROWS
    used = (valid[:, 0, :] > 0).astype(jnp.int32)
    before = jnp.sum(
        used[:, None, :] * (jnp.arange(8)[None, :, None] > jnp.arange(8)[None, None, :]), -1
    )
    hit = used[:, :, None] * (before[:, :, None] == jnp.arange(8)[None, None, :])
    listed = jnp.sum(index[:, :, None] * hit, 1)
    own = (jnp.arange(ROWS, dtype=jnp.int32) + ROWS)[:, None]
    return jnp.concatenate([own, listed], 1).astype(jnp.int32), (
        1 + jnp.sum(used, 1)
    ).astype(jnp.int32)


def per_device(
    features, norm_gain, query_weight, key_weight, value_weight, output_weight, adjacency, valid
):
    flat = features.reshape(ROWS * CS, D)
    n = lax.axis_size("z") * lax.axis_size("x") * 2
    above = lax.ppermute(flat, NODES, [(i, i + 1) for i in range(n - 1)])
    below = lax.ppermute(flat, NODES, [(i + 1, i) for i in range(n - 1)])
    gathered = []
    for weight in (key_weight, value_weight, query_weight, output_weight):
        mine, other = gather_pieces(half_rows(weight))
        gathered.append(place_halves(weight, mine, other))
    wk, wv, wq, wo = gathered
    gain = norm_gain.reshape(1, D)
    node = lax.axis_index(NODES)
    slots, counts = key_slots(adjacency, valid, node)
    own = ROWS * CS
    kv = project("own_kv", flat, gain, [wk, wv], (1.0, 1.0), 3 * own, own)
    (queries,) = project("own_q", flat, gain, [wq], (QSCALE,), own, 0)
    kv = project("above_kv", above, gain, [wk, wv], (1.0, 1.0), 3 * own, 0, kv)
    keys, values = project("below_kv", below, gain, [wk, wv], (1.0, 1.0), 3 * own, 2 * own, kv)
    window = (3 * ROWS, CS, D)
    out = attend(
        slots,
        counts,
        queries.reshape(ROWS, CS, D),
        keys.reshape(window),
        values.reshape(window),
        flat,
        wo,
    )
    return out.reshape(ROWS, 1, CS, D)


def solution(mesh):
    nodes, fsdp = mesh.devices.shape
    split = Mesh(mesh.devices.reshape(nodes // 8, 4, 2, fsdp), NODES + ("fsdp",))
    in_specs = (
        P(NODES, "fsdp", None, None),
        P(),
        P("fsdp", None),
        P("fsdp", None),
        P("fsdp", None),
        P("fsdp", None),
        P(NODES, "fsdp", None),
        P(NODES, "fsdp", None),
    )
    out_specs = P(NODES, "fsdp", None, None)
    return jax.shard_map(
        per_device, mesh=split, in_specs=in_specs, out_specs=out_specs, check_vma=False
    )
```

time: 496 us -> 155 us (0.31)
  the two profiles are of different devices: /device:TPU:103 before, /device:TPU:225 now
where the time goes in v1:
time: 155 us
  Pallas kernels  79.5 us (51%)
  starting transfers between devices  38.9 us (25%)
  local copies, waits for them, and re-layouts  29.2 us (19%)
  waiting for transfers between devices  3.09 us (2%)
  other arithmetic  3.03 us (2%)
    pallas_call x1, Pallas kernels, attend(): pl.pallas_call(functools.partial(attend_kernel, n_pieces=n), out_shape=ja...  45.2 us
    pallas_call x4, Pallas kernels, project(): pl.pallas_call(kernel, out_shape=[jax.ShapeDtypeStruct((total, D), BF)] *...  34.4 us
    unnamed x88, local copies, waits for them, and re-layouts  21 us
    ppermute x16, starting transfers between devices, swap_cores(): return lax.ppermute(t, 'core', [(0, 1), (1, 0)])  10.5 us
    ppermute x4, starting transfers between devices, gather_pieces(): d = lax.ppermute(b[half:], 'fsdp', down)  9.57 us
    ppermute x4, starting transfers between devices, gather_pieces(): b = lax.ppermute(shards, 'fsdp', down)  8.25 us
    ppermute x1, starting transfers between devices, per_device(): above = lax.ppermute(flat, NODES, [(i, i + 1) for i in range(n - 1)])  5.97 us
    dynamic_slice x4, local copies, waits for them, and re-layouts, half_rows(): return lax.dynamic_slice_in_dim(weight, core * (SHARD // 2), SHARD // 2, 0)  5.27 us
  transfers between devices with their start and end apart: 34, of which 5 were waited for; matrix products, arithmetic and copies ran while one was open for 7% of the time, Pallas kernels for 22%

profile of v1, /device:TPU:225, one launch (start us, length us, event | category | flops | bytes accessed | tf_op | source)
XLA Modules:
  0.0 154.5 jit_solution(8289693378837607506)
XLA Ops:
  1.0 1.4 collective-permute-start.9
  2.3 1.5 collective-permute-start.10
  4.9 2.7 %collective-permute-start.18 = (bf16[128,1024]{1,0:T(8,128)(2,1)S(1)}, bf16[128,1024]{1,0:T(8,128)(2,1)S(1)}, u32[]{:S(2)}, u32[]{:S(2)}) collective-permute-start(bf16[128,1024]{1,0:T(8,128)(2,1)S(1)} %constant_dynamic-slice_fusion.1), channel_id=1, source_target_pairs={{1,0},{2,1},{3,2},{0,3},{5,4},{6,5},{7,6},{4,7},{9,8},{10,9},{11,1... | collective-permute-start | bytes 786440 | tf_op jit(solution)/shard_map/ppermute | solution.py:32
  7.6 1.7 %constant_dynamic-slice_fusion.3 = bf16[128,1024]{1,0:T(8,128)(2,1)} fusion(bf16[256,1024]{1,0:T(8,128)(2,1)} %refs_0_.5, s32[]{:T(128)S(6)} %select_n.82), kind=kLoop, calls=%fused_computation.14 | loop fusion | bytes 524292 | tf_op jit(solution)/shard_map/dynamic_slice | solution.py:40
  9.3 1.7 %constant_dynamic-slice_fusion = bf16[128,1024]{1,0:T(8,128)(2,1)} fusion(bf16[256,1024]{1,0:T(8,128)(2,1)} %refs_0_.9, s32[]{:T(128)S(6)} %select_n.82), kind=kLoop, calls=%fused_computation.11 | loop fusion | bytes 524292 | tf_op jit(solution)/shard_map/dynamic_slice | solution.py:40
  10.9 2.7 %collective-permute-start.1 = (bf16[128,1024]{1,0:T(8,128)(2,1)}, bf16[128,1024]{1,0:T(8,128)(2,1)}, u32[]{:S(2)}, u32[]{:S(2)}) collective-permute-start(bf16[128,1024]{1,0:T(8,128)(2,1)} %constant_dynamic-slice_fusion.3), channel_id=1, source_target_pairs={{1,0},{2,1},{3,2},{0,3},{5,4},{6,5},{7,6},{4,7},{9,8},{10,9},{11,1... | collective-permute-start | bytes 786440 | tf_op jit(solution)/shard_map/ppermute | solution.py:32
  13.6 1.6 %collective-permute-done.17.refs_10_ = bf16[128,1024]{1,0:T(8,128)(2,1)S(1)} collective-permute-done((bf16[128,1024]{1,0:T(8,128)(2,1)S(1)}, bf16[128,1024]{1,0:T(8,128)(2,1)S(1)}, u32[]{:S(2)}, u32[]{:S(2)}) %collective-permute-start.17) | collective-permute-done | bytes 262176 | tf_op jit(solution)/shard_map/ppermute | solution.py:31
  15.2 1.4 collective-permute-start.27
  16.6 6.0 %collective-permute-start.25 = (bf16[1024,1024]{1,0:T(8,128)(2,1)}, bf16[1024,1024]{1,0:T(8,128)(2,1)S(1)}, u32[]{:S(2)}, u32[]{:S(2)}) collective-permute-start(bf16[1024,1024]{1,0:T(8,128)(2,1)} %bitcast.28), channel_id=1, source_target_pairs={{0,4},{4,8},{8,12},{12,16},{16,20},{20,24},{24,28},{28,32},{32,36}... | collective-permute-start | bytes 6291464 | tf_op jit(solution)/shard_map/ppermute | solution.py:281
  23.5 2.9 %collective-permute-start.8 = (bf16[1024,1024]{1,0:T(8,128)(2,1)}, bf16[1024,1024]{1,0:T(8,128)(2,1)}, u32[]{:S(2)}, u32[]{:S(2)}) collective-permute-start(bf16[1024,1024]{1,0:T(8,128)(2,1)} %bitcast.29), channel_id=1, source_target_pairs={{4,0},{8,4},{12,8},{16,12},{20,16},{24,20},{28,24},{32,28},{36,32}... | collective-permute-start | bytes 6291464 | tf_op jit(solution)/shard_map/ppermute | solution.py:282
  26.5 2.5 %collective-permute-start.12 = (bf16[64,1024]{1,0:T(8,128)(2,1)S(1)}, bf16[64,1024]{1,0:T(8,128)(2,1)S(1)}, u32[]{:S(2)}, u32[]{:S(2)}) collective-permute-start(bf16[64,1024]{1,0:T(8,128)(2,1)S(1)} %slice.35), channel_id=1, source_target_pairs={{1,0},{2,1},{3,2},{0,3},{5,4},{6,5},{7,6},{4,7},{9,8},{10,9},{11,1... | collective-permute-start | bytes 393224 | tf_op jit(solution)/shard_map/ppermute | solution.py:34
  29.5 2.3 %collective-permute-start.20 = (bf16[64,1024]{1,0:T(8,128)(2,1)S(1)}, bf16[64,1024]{1,0:T(8,128)(2,1)S(1)}, u32[]{:S(2)}, u32[]{:S(2)}) collective-permute-start(bf16[64,1024]{1,0:T(8,128)(2,1)S(1)} %slice.37), channel_id=1, source_target_pairs={{1,0},{2,1},{3,2},{0,3},{5,4},{6,5},{7,6},{4,7},{9,8},{10,9},{11,1... | collective-permute-start | bytes 393224 | tf_op jit(solution)/shard_map/ppermute | solution.py:34
  34.4 1.9 %collective-permute-start.3 = (bf16[64,1024]{1,0:T(8,128)(2,1)S(1)}, bf16[64,1024]{1,0:T(8,128)(2,1)}, u32[]{:S(2)}, u32[]{:S(2)}) collective-permute-start(bf16[64,1024]{1,0:T(8,128)(2,1)S(1)} %slice.33), channel_id=1, source_target_pairs={{1,0},{2,1},{3,2},{0,3},{5,4},{6,5},{7,6},{4,7},{9,8},{10,9},{11,1... | collective-permute-start | bytes 393224 | tf_op jit(solution)/shard_map/ppermute | solution.py:34
  36.3 3.2 %collective-permute-start.15 = (bf16[64,1024]{1,0:T(8,128)(2,1)S(1)}, bf16[64,1024]{1,0:T(8,128)(2,1)S(1)}, u32[]{:S(2)}, u32[]{:S(2)}) collective-permute-start(bf16[64,1024]{1,0:T(8,128)(2,1)S(1)} %collective-permute-done.11.refs_3_), channel_id=1, source_target_pairs={{0,4},{4,0},{1,5},{5,1},{2,6},{6,2},{3,7},{7,3},{8,12},{12,8},{9,1... | collective-permute-start | bytes 393224 | tf_op jit(solution)/shard_map/ppermute | solution.py:24
  39.5 3.0 %collective-permute-start.13 = (bf16[128,1024]{1,0:T(8,128)(2,1)S(1)}, bf16[128,1024]{1,0:T(8,128)(2,1)S(1)}, u32[]{:S(2)}, u32[]{:S(2)}) collective-permute-start(bf16[128,1024]{1,0:T(8,128)(2,1)S(1)} %collective-permute-done.9.refs_1_), channel_id=1, source_target_pairs={{0,4},{4,0},{1,5},{5,1},{2,6},{6,2},{3,7},{7,3},{8,12},{12,8},{9,1... | collective-permute-start | bytes 786440 | tf_op jit(solution)/shard_map/ppermute | solution.py:24
  55.2 1.0 copy-done.3
  64.2 1.6 %copy-done.35 = bf16[8,1,128,1024]{3,2,1,0:T(8,128)(2,1)S(1)} copy-done((bf16[8,1,128,1024]{3,2,1,0:T(8,128)(2,1)S(1)}, bf16[8,1,128,1024]{3,2,1,0:T(8,128)(2,1)}, u32[]{:S(2)}) %copy-start.35) | copy-done | bytes 2097176
  65.8 9.4 %own_kv.1 = (bf16[3072,1024]{1,0:T(8,128)(2,1)S(1)}, bf16[3072,1024]{1,0:T(8,128)(2,1)}) custom-call(s32[18]{0:T(128)S(1)} %stack.32.starts, bf16[1024,1024]{1,0:T(8,128)(2,1)S(1)} %bitcast.31, f32[1,1024]{1,0:T(1,128)S(1)} %bitcast.24, bf16[256,1024]{1,0:T(8,128)(2,1)S(1)} %copy-done.1, bf16[128,1024]{1,0:T(8,128)(2,1)S(1)} %collective-permute-done.9.refs_1_, ...), custom_call_target="tpu_custom_call" | custom-call | flops 4294967296 | bytes 10485760 | tf_op jit(solution)/shard_map/own_kv/pallas_call | solution.py:105
  75.5 2.9 %collective-permute-start.29 = (bf16[64,1024]{1,0:T(8,128)(2,1)S(1)}, bf16[64,1024]{1,0:T(8,128)(2,1)S(1)}, u32[]{:S(2)}, u32[]{:S(2)}) collective-permute-start(bf16[64,1024]{1,0:T(8,128)(2,1)S(1)} %slice.39), channel_id=1, source_target_pairs={{1,0},{2,1},{3,2},{0,3},{5,4},{6,5},{7,6},{4,7},{9,8},{10,9},{11,1... | collective-permute-start | bytes 393224 | tf_op jit(solution)/shard_map/ppermute | solution.py:34
  79.1 5.1 %own_q.1 = bf16[1024,1024]{1,0:T(8,128)(2,1)S(1)} custom-call(s32[9]{0:T(128)S(1)} %stack.31.starts, bf16[1024,1024]{1,0:T(8,128)(2,1)S(1)} %bitcast.32, f32[1,1024]{1,0:T(1,128)S(1)} %bitcast.25, bf16[256,1024]{1,0:T(8,128)(2,1)S(1)} %copy-done.29, bf16[128,1024]{1,0:T(8,128)(2,1)S(1)} %copy-done.31, bf16[128,1024]{1,0:T(8,128)(2,1)} %collective-permute-done.1.refs_2_, ...), custom_call_target="tpu_custom_call" | custom-call | flops 2147483648 | bytes 6291456 | tf_op jit(solution)/shard_map/own_q/pallas_call | solution.py:105
  85.2 9.4 %above_kv.1 = (bf16[3072,1024]{1,0:T(8,128)(2,1)S(1)}, bf16[3072,1024]{1,0:T(8,128)(2,1)}) custom-call(s32[18]{0:T(128)S(1)} %stack.32.starts, bf16[1024,1024]{1,0:T(8,128)(2,1)S(1)} %collective-permute-done.25.x_ref, f32[1,1024]{1,0:T(1,128)S(1)} %bitcast.26, bf16[256,1024]{1,0:T(8,128)(2,1)S(1)} %copy-done.2, ...), custom_call_target="tpu_custom_call", output_to_operand_aliasing={{0}: (21, {}), {1}: (22, {})} | custom-call | flops 4294967296 | bytes 10485760 | tf_op jit(solution)/shard_map/above_kv/pallas_call | solution.py:105
  94.7 10.4 %below_kv.1 = (bf16[3072,1024]{1,0:T(8,128)(2,1)S(1)}, bf16[3072,1024]{1,0:T(8,128)(2,1)}) custom-call(s32[18]{0:T(128)S(1)} %stack.32.starts, bf16[1024,1024]{1,0:T(8,128)(2,1)} %collective-permute-done.8.x_ref, f32[1,1024]{1,0:T(1,128)S(1)} %bitcast.27, bf16[256,1024]{1,0:T(8,128)(2,1)S(1)} %copy-done.2, ...), custom_call_target="tpu_custom_call", output_to_operand_aliasing={{0}: (21, {}), {1}: (22, {})} | custom-call | flops 4294967296 | bytes 10485760 | tf_op jit(solution)/shard_map/below_kv/pallas_call | solution.py:105
  105.1 2.7 %copy-done = bf16[3072,1024]{1,0:T(8,128)(2,1)} copy-done((bf16[3072,1024]{1,0:T(8,128)(2,1)}, bf16[3072,1024]{1,0:T(8,128)(2,1)S(1)}, u32[]{:S(2)}) %copy-start) | copy-done | bytes 6291480
  109.2 45.2 %attend.1 = bf16[1024,1024]{1,0:T(8,128)(2,1)} custom-call(s32[8,9]{1,0:T(8,128)} %pad_add_fusion.slots, s32[8]{0:T(128)} %broadcast_add_fusion.counts, s32[9]{0:T(128)} %copy-done.34, bf16[8,128,1024]{2,1,0:T(8,128)(2,1)} %bitcast.33, bf16[24,128,1024]{2,1,0:T(8,128)(2,1)} %bitcast.23, bf16[24,128,1024]{2,1,0:T(8,128)(2,1)} %bitcast.34, ...), custom_call_target="tpu_custom_call" | custom-call | flops 21474836480 | bytes 20971520 | tf_op jit(solution)/shard_map/attend/pallas_call | solution.py:233
  (160 shorter events, 29.7 us)
Async XLA Ops:
  1.0 10.0 %collective-permute-start.9 = (bf16[128,1024]{1,0:T(8,128)(2,1)S(1)}, bf16[128,1024]{1,0:T(8,128)(2,1)S(1)}, u32[]{:S(2)}, u32[]{:S(2)}) collective-permute-start(bf16[128,1024]{1,0:T(8,128)(2,1)S(1)} %constant_dynamic-slice_fusion.2), channel_id=1, source_target_pairs={{0,1},{1,2},{2,3},{3,0},{4,5},{5,6},{6,7},{7,4},{8,9},{9,10},{10,1... | collective-permute-start | bytes 786440 | tf_op jit(solution)/shard_map/ppermute | solution.py:31
  2.3 11.3 %collective-permute-start.10 = (bf16[128,1024]{1,0:T(8,128)(2,1)S(1)}, bf16[128,1024]{1,0:T(8,128)(2,1)S(1)}, u32[]{:S(2)}, u32[]{:S(2)}) collective-permute-start(bf16[128,1024]{1,0:T(8,128)(2,1)S(1)} %constant_dynamic-slice_fusion.2), channel_id=1, source_target_pairs={{1,0},{2,1},{3,2},{0,3},{5,4},{6,5},{7,6},{4,7},{9,8},{10,9},{11,1... | collective-permute-start | bytes 786440 | tf_op jit(solution)/shard_map/ppermute | solution.py:32
  4.8 10.3 %collective-permute-start.17 = (bf16[128,1024]{1,0:T(8,128)(2,1)S(1)}, bf16[128,1024]{1,0:T(8,128)(2,1)S(1)}, u32[]{:S(2)}, u32[]{:S(2)}) collective-permute-start(bf16[128,1024]{1,0:T(8,128)(2,1)S(1)} %constant_dynamic-slice_fusion.1), channel_id=1, source_target_pairs={{0,1},{1,2},{2,3},{3,0},{4,5},{5,6},{6,7},{7,4},{8,9},{9,10},{10,1... | collective-permute-start | bytes 786440 | tf_op jit(solution)/shard_map/ppermute | solution.py:31
  4.9 11.6 %collective-permute-start.18 = (bf16[128,1024]{1,0:T(8,128)(2,1)S(1)}, bf16[128,1024]{1,0:T(8,128)(2,1)S(1)}, u32[]{:S(2)}, u32[]{:S(2)}) collective-permute-start(bf16[128,1024]{1,0:T(8,128)(2,1)S(1)} %constant_dynamic-slice_fusion.1), channel_id=1, source_target_pairs={{1,0},{2,1},{3,2},{0,3},{5,4},{6,5},{7,6},{4,7},{9,8},{10,9},{11,1... | collective-permute-start | bytes 786440 | tf_op jit(solution)/shard_map/ppermute | solution.py:32
  9.3 13.3 %collective-permute-start = (bf16[128,1024]{1,0:T(8,128)(2,1)}, bf16[128,1024]{1,0:T(8,128)(2,1)S(1)}, u32[]{:S(2)}, u32[]{:S(2)}) collective-permute-start(bf16[128,1024]{1,0:T(8,128)(2,1)} %constant_dynamic-slice_fusion.3), channel_id=1, source_target_pairs={{0,1},{1,2},{2,3},{3,0},{4,5},{5,6},{6,7},{7,4},{8,9},{9,10},{10,1... | collective-permute-start | bytes 786440 | tf_op jit(solution)/shard_map/ppermute | solution.py:31
  10.9 12.5 %collective-permute-start.1 = (bf16[128,1024]{1,0:T(8,128)(2,1)}, bf16[128,1024]{1,0:T(8,128)(2,1)}, u32[]{:S(2)}, u32[]{:S(2)}) collective-permute-start(bf16[128,1024]{1,0:T(8,128)(2,1)} %constant_dynamic-slice_fusion.3), channel_id=1, source_target_pairs={{1,0},{2,1},{3,2},{0,3},{5,4},{6,5},{7,6},{4,7},{9,8},{10,9},{11,1... | collective-permute-start | bytes 786440 | tf_op jit(solution)/shard_map/ppermute | solution.py:32
  13.6 12.9 %collective-permute-start.26 = (bf16[128,1024]{1,0:T(8,128)(2,1)}, bf16[128,1024]{1,0:T(8,128)(2,1)}, u32[]{:S(2)}, u32[]{:S(2)}) collective-permute-start(bf16[128,1024]{1,0:T(8,128)(2,1)} %constant_dynamic-slice_fusion), channel_id=1, source_target_pairs={{0,1},{1,2},{2,3},{3,0},{4,5},{5,6},{6,7},{7,4},{8,9},{9,10},{10,1... | collective-permute-start | bytes 786440 | tf_op jit(solution)/shard_map/ppermute | solution.py:31
  15.2 13.9 %collective-permute-start.27 = (bf16[128,1024]{1,0:T(8,128)(2,1)}, bf16[128,1024]{1,0:T(8,128)(2,1)}, u32[]{:S(2)}, u32[]{:S(2)}) collective-permute-start(bf16[128,1024]{1,0:T(8,128)(2,1)} %constant_dynamic-slice_fusion), channel_id=1, source_target_pairs={{1,0},{2,1},{3,2},{0,3},{5,4},{6,5},{7,6},{4,7},{9,8},{10,9},{11,1... | collective-permute-start | bytes 786440 | tf_op jit(solution)/shard_map/ppermute | solution.py:32
  16.6 68.3 %collective-permute-start.25 = (bf16[1024,1024]{1,0:T(8,128)(2,1)}, bf16[1024,1024]{1,0:T(8,128)(2,1)S(1)}, u32[]{:S(2)}, u32[]{:S(2)}) collective-permute-start(bf16[1024,1024]{1,0:T(8,128)(2,1)} %bitcast.28), channel_id=1, source_target_pairs={{0,4},{4,8},{8,12},{12,16},{16,20},{20,24},{24,28},{28,32},{32,36}... | collective-permute-start | bytes 6291464 | tf_op jit(solution)/shard_map/ppermute | solution.py:281
  22.6 6.9 %collective-permute-start.11 = (bf16[64,1024]{1,0:T(8,128)(2,1)S(1)}, bf16[64,1024]{1,0:T(8,128)(2,1)S(1)}, u32[]{:S(2)}, u32[]{:S(2)}) collective-permute-start(bf16[64,1024]{1,0:T(8,128)(2,1)S(1)} %slice.34), channel_id=1, source_target_pairs={{0,1},{1,2},{2,3},{3,0},{4,5},{5,6},{6,7},{7,4},{8,9},{9,10},{10,1... | collective-permute-start | bytes 393224 | tf_op jit(solution)/shard_map/ppermute | solution.py:33
  23.5 71.2 %collective-permute-start.8 = (bf16[1024,1024]{1,0:T(8,128)(2,1)}, bf16[1024,1024]{1,0:T(8,128)(2,1)}, u32[]{:S(2)}, u32[]{:S(2)}) collective-permute-start(bf16[1024,1024]{1,0:T(8,128)(2,1)} %bitcast.29), channel_id=1, source_target_pairs={{4,0},{8,4},{12,8},{16,12},{20,16},{24,20},{28,24},{32,28},{36,32}... | collective-permute-start | bytes 6291464 | tf_op jit(solution)/shard_map/ppermute | solution.py:282
  26.5 7.0 %collective-permute-start.12 = (bf16[64,1024]{1,0:T(8,128)(2,1)S(1)}, bf16[64,1024]{1,0:T(8,128)(2,1)S(1)}, u32[]{:S(2)}, u32[]{:S(2)}) collective-permute-start(bf16[64,1024]{1,0:T(8,128)(2,1)S(1)} %slice.35), channel_id=1, source_target_pairs={{1,0},{2,1},{3,2},{0,3},{5,4},{6,5},{7,6},{4,7},{9,8},{10,9},{11,1... | collective-permute-start | bytes 393224 | tf_op jit(solution)/shard_map/ppermute | solution.py:34
  34.4 8.1 %collective-permute-start.3 = (bf16[64,1024]{1,0:T(8,128)(2,1)S(1)}, bf16[64,1024]{1,0:T(8,128)(2,1)}, u32[]{:S(2)}, u32[]{:S(2)}) collective-permute-start(bf16[64,1024]{1,0:T(8,128)(2,1)S(1)} %slice.33), channel_id=1, source_target_pairs={{1,0},{2,1},{3,2},{0,3},{5,4},{6,5},{7,6},{4,7},{9,8},{10,9},{11,1... | collective-permute-start | bytes 393224 | tf_op jit(solution)/shard_map/ppermute | solution.py:34
  36.3 6.9 %collective-permute-start.15 = (bf16[64,1024]{1,0:T(8,128)(2,1)S(1)}, bf16[64,1024]{1,0:T(8,128)(2,1)S(1)}, u32[]{:S(2)}, u32[]{:S(2)}) collective-permute-start(bf16[64,1024]{1,0:T(8,128)(2,1)S(1)} %collective-permute-done.11.refs_3_), channel_id=1, source_target_pairs={{0,4},{4,0},{1,5},{5,1},{2,6},{6,2},{3,7},{7,3},{8,12},{12,8},{9,1... | collective-permute-start | bytes 393224 | tf_op jit(solution)/shard_map/ppermute | solution.py:24
  39.5 9.9 %collective-permute-start.13 = (bf16[128,1024]{1,0:T(8,128)(2,1)S(1)}, bf16[128,1024]{1,0:T(8,128)(2,1)S(1)}, u32[]{:S(2)}, u32[]{:S(2)}) collective-permute-start(bf16[128,1024]{1,0:T(8,128)(2,1)S(1)} %collective-permute-done.9.refs_1_), channel_id=1, source_target_pairs={{0,4},{4,0},{1,5},{5,1},{2,6},{6,2},{3,7},{7,3},{8,12},{12,8},{9,1... | collective-permute-start | bytes 786440 | tf_op jit(solution)/shard_map/ppermute | solution.py:24
  53.4 22.1 %collective-permute-start.4 = (bf16[128,1024]{1,0:T(8,128)(2,1)}, bf16[128,1024]{1,0:T(8,128)(2,1)S(1)}, u32[]{:S(2)}, u32[]{:S(2)}) collective-permute-start(bf16[128,1024]{1,0:T(8,128)(2,1)} %copy-done.30), channel_id=1, source_target_pairs={{0,4},{4,0},{1,5},{5,1},{2,6},{6,2},{3,7},{7,3},{8,12},{12,8},{9,1... | collective-permute-start | bytes 786440 | tf_op jit(solution)/shard_map/ppermute | solution.py:24
  53.7 24.7 %collective-permute-start.5 = (bf16[128,1024]{1,0:T(8,128)(2,1)}, bf16[128,1024]{1,0:T(8,128)(2,1)S(1)}, u32[]{:S(2)}, u32[]{:S(2)}) collective-permute-start(bf16[128,1024]{1,0:T(8,128)(2,1)} %collective-permute-done.1.refs_2_), channel_id=1, source_target_pairs={{0,4},{4,0},{1,5},{5,1},{2,6},{6,2},{3,7},{7,3},{8,12},{12,8},{9,1... | collective-permute-start | bytes 786440 | tf_op jit(solution)/shard_map/ppermute | solution.py:24
  54.0 21.3 %collective-permute-start.7 = (bf16[64,1024]{1,0:T(8,128)(2,1)}, bf16[64,1024]{1,0:T(8,128)(2,1)S(1)}, u32[]{:S(2)}, u32[]{:S(2)}) collective-permute-start(bf16[64,1024]{1,0:T(8,128)(2,1)} %collective-permute-done.3.refs_4_), channel_id=1, source_target_pairs={{0,4},{4,0},{1,5},{5,1},{2,6},{6,2},{3,7},{7,3},{8,12},{12,8},{9,1... | collective-permute-start | bytes 393224 | tf_op jit(solution)/shard_map/ppermute | solution.py:24
  75.4 8.8 %collective-permute-start.28 = (bf16[64,1024]{1,0:T(8,128)(2,1)S(1)}, bf16[64,1024]{1,0:T(8,128)(2,1)S(1)}, u32[]{:S(2)}, u32[]{:S(2)}) collective-permute-start(bf16[64,1024]{1,0:T(8,128)(2,1)S(1)} %slice.38), channel_id=1, source_target_pairs={{0,1},{1,2},{2,3},{3,0},{4,5},{5,6},{6,7},{7,4},{8,9},{9,10},{10,1... | collective-permute-start | bytes 393224 | tf_op jit(solution)/shard_map/ppermute | solution.py:33
  75.5 8.9 %collective-permute-start.29 = (bf16[64,1024]{1,0:T(8,128)(2,1)S(1)}, bf16[64,1024]{1,0:T(8,128)(2,1)S(1)}, u32[]{:S(2)}, u32[]{:S(2)}) collective-permute-start(bf16[64,1024]{1,0:T(8,128)(2,1)S(1)} %slice.39), channel_id=1, source_target_pairs={{1,0},{2,1},{3,2},{0,3},{5,4},{6,5},{7,6},{4,7},{9,8},{10,9},{11,1... | collective-permute-start | bytes 393224 | tf_op jit(solution)/shard_map/ppermute | solution.py:34
  78.4 29.5 %collective-permute-start.30 = (bf16[128,1024]{1,0:T(8,128)(2,1)}, bf16[128,1024]{1,0:T(8,128)(2,1)S(1)}, u32[]{:S(2)}, u32[]{:S(2)}) collective-permute-start(bf16[128,1024]{1,0:T(8,128)(2,1)} %collective-permute-done.26.refs_1_), channel_id=1, source_target_pairs={{0,4},{4,0},{1,5},{5,1},{2,6},{6,2},{3,7},{7,3},{8,12},{12,8},{9,1... | collective-permute-start | bytes 786440 | tf_op jit(solution)/shard_map/ppermute | solution.py:24
  84.2 23.6 %collective-permute-start.31 = (bf16[128,1024]{1,0:T(8,128)(2,1)}, bf16[128,1024]{1,0:T(8,128)(2,1)S(1)}, u32[]{:S(2)}, u32[]{:S(2)}) collective-permute-start(bf16[128,1024]{1,0:T(8,128)(2,1)} %collective-permute-done.27.refs_2_), channel_id=1, source_target_pairs={{0,4},{4,0},{1,5},{5,1},{2,6},{6,2},{3,7},{7,3},{8,12},{12,8},{9,1... | collective-permute-start | bytes 786440 | tf_op jit(solution)/shard_map/ppermute | solution.py:24
  84.4 23.5 %collective-permute-start.32 = (bf16[64,1024]{1,0:T(8,128)(2,1)S(1)}, bf16[64,1024]{1,0:T(8,128)(2,1)S(1)}, u32[]{:S(2)}, u32[]{:S(2)}) collective-permute-start(bf16[64,1024]{1,0:T(8,128)(2,1)S(1)} %collective-permute-done.28.refs_3_), channel_id=1, source_target_pairs={{0,4},{4,0},{1,5},{5,1},{2,6},{6,2},{3,7},{7,3},{8,12},{12,8},{9,1... | collective-permute-start | bytes 393224 | tf_op jit(solution)/shard_map/ppermute | solution.py:24
  84.8 23.0 %collective-permute-start.33 = (bf16[64,1024]{1,0:T(8,128)(2,1)S(1)}, bf16[64,1024]{1,0:T(8,128)(2,1)S(1)}, u32[]{:S(2)}, u32[]{:S(2)}) collective-permute-start(bf16[64,1024]{1,0:T(8,128)(2,1)S(1)} %collective-permute-done.29.refs_4_), channel_id=1, source_target_pairs={{0,4},{4,0},{1,5},{5,1},{2,6},{6,2},{3,7},{7,3},{8,12},{12,8},{9,1... | collective-permute-start | bytes 393224 | tf_op jit(solution)/shard_map/ppermute | solution.py:24
  (54 other events, 291.3 us)

commit v2 on v1

v2 whole, which is shorter than its diff:
```python
import functools

import jax
import jax.numpy as jnp
from jax import lax
from jax.experimental import pallas as pl
from jax.experimental.pallas import tpu as pltpu
from jax.sharding import Mesh
from jax.sharding import PartitionSpec as P

BF = jnp.bfloat16
F32 = jnp.float32
NODES = ("z", "x", "core")
HSIZE = 64
QSCALE = 1.4426950408889634 / HSIZE**0.5
ROWS = 8
CS = 128
D = 1024
TILE = 256
SHARD = 256
WIDE = 512


def swap_cores(t):
    return lax.ppermute(t, "core", [(0, 1), (1, 0)])


def split_kernel(core, k_ref, v_ref, q_ref, o_ref, first, second):
    half = SHARD // 2
    for i, ref in enumerate((k_ref, v_ref, q_ref)):
        first[i * half : (i + 1) * half] = ref[...]
    second[...] = o_ref[...]


def split_rows(weights, core):
    half = SHARD // 2
    return pl.pallas_call(
        split_kernel,
        out_shape=[
            jax.ShapeDtypeStruct((3 * half, D), BF),
            jax.ShapeDtypeStruct((half, D), BF),
        ],
        grid_spec=pltpu.PrefetchScalarGridSpec(
            num_scalar_prefetch=1,
            grid=(1,),
            in_specs=[pl.BlockSpec((half, D), lambda i, c: (c[0], 0))] * 4,
            out_specs=[
                pl.BlockSpec((3 * half, D), lambda i, c: (0, 0)),
                pl.BlockSpec((half, D), lambda i, c: (0, 0)),
            ],
        ),
        name="split_rows",
    )(core.reshape(1), *weights)


UP = [(i, (i + 1) % 4) for i in range(4)]
DOWN = [((i + 1) % 4, i) for i in range(4)]


def relayed_rows(part, after):
    half = part.shape[0] // 2
    below = lax.ppermute(part, "fsdp", UP)
    above = lax.ppermute(part, "fsdp", DOWN)
    below, above, after = lax.optimization_barrier((below, above, after))
    far = (
        lax.ppermute(below[:half], "fsdp", UP),
        lax.ppermute(above[half:], "fsdp", DOWN),
    )
    mine = (below, above) + far
    return mine + tuple(swap_cores(t) for t in mine), after


def direct_rows(part):
    return [
        lax.ppermute(part, "fsdp", [(i, (i + k) % 4) for i in range(4)]) for k in (1, 3, 2)
    ]


def piece_plan(index, count):
    h = SHARD // 2
    if count == 1:
        return [(i, 0, h, i + 1, 0) for i in range(6)]
    total = count * h
    plan = []
    for side in range(2):
        plan.append((4 * side, index * h, h, 1 + 3 * side, 0))
        plan.append((4 * side + 1, index * h, h, 2 + 3 * side, 0))
        for part, (lo, hi) in enumerate(((0, total // 2), (total // 2, total))):
            first = max(lo, index * h)
            last = min(hi, (index + 1) * h)
            if first < last:
                plan.append(
                    (4 * side + 2 + part, first - lo, last - first, 3 + 3 * side, first - index * h)
                )
    return plan


def place_starts(y, core):
    h = SHARD // 2
    starts = [y * SHARD]
    for side in (core, 1 - core):
        starts += [(y + k) % 4 * SHARD + side * h for k in (3, 1, 2)]
    return jnp.stack(starts).astype(jnp.int32)


def weight_copies(starts, shard, arrays, index, count, target, sems):
    row = pl.multiple_of(starts[0], SHARD)
    copies = [pltpu.make_async_copy(shard, target.at[pl.ds(row, SHARD)], sems.at[0])]
    for n, (array, first, rows, place, offset) in enumerate(piece_plan(index, count)):
        row = pl.multiple_of(starts[place] + offset, 64)
        copies.append(
            pltpu.make_async_copy(
                arrays[array].at[pl.ds(first, rows)],
                target.at[pl.ds(row, rows)],
                sems.at[n + 1],
            )
        )
    return copies


PIECES = 9


def project_kernel(starts, x_ref, gain_ref, *refs, count, stacked, scales):
    shards, arrays, refs = refs[:count], refs[count : count + 8], refs[count + 8 :]
    outs, (weights, sems) = refs[:count], refs[count:]
    step = pl.program_id(0)

    def copies(w):
        return weight_copies(starts, shards[w], arrays, w, stacked, weights.at[w], sems.at[w])

    @pl.when(step == 0)
    def _():
        for w in range(count):
            for c in copies(w):
                c.start()

    wide = x_ref[...].astype(F32)
    mean = jnp.mean(wide * wide, axis=-1, keepdims=True)
    normed = (wide * lax.rsqrt(mean + 1e-06) * gain_ref[...]).astype(BF)
    for w in range(count):

        @pl.when(step == 0)
        def _():
            for c in copies(w):
                c.wait()

        got = jnp.dot(normed, weights[w], preferred_element_type=F32)
        if scales[w] != 1.0:
            got = got * scales[w]
        outs[w][...] = got.astype(BF)


def project(name, x, gain, starts, shards, arrays, stacked, scales):
    count = len(shards)
    rows = x.shape[0]
    return pl.pallas_call(
        functools.partial(project_kernel, count=count, stacked=stacked, scales=scales),
        out_shape=[jax.ShapeDtypeStruct((rows, D), BF)] * count,
        grid_spec=pltpu.PrefetchScalarGridSpec(
            num_scalar_prefetch=1,
            grid=(rows // TILE,),
            in_specs=[
                pl.BlockSpec((TILE, D), lambda i, s: (i, 0)),
                pl.BlockSpec((1, D), lambda i, s: (0, 0)),
            ]
            + [pl.BlockSpec(memory_space=pltpu.HBM)] * (count + 8),
            out_specs=[pl.BlockSpec((TILE, D), lambda i, s: (i, 0))] * count,
            scratch_shapes=[
                pltpu.VMEM((count, D, D), BF),
                pltpu.SemaphoreType.DMA((count, PIECES)),
            ],
        ),
        compiler_params=pltpu.CompilerParams(vmem_limit_bytes=56 << 20),
        cost_estimate=pl.CostEstimate(
            flops=2 * rows * D * D * count * 16,
            bytes_accessed=2 * (rows * D * (1 + count) + count * D * D),
            transcendentals=0,
        ),
        name=name,
    )(starts, x, gain, *shards, *arrays)


def attend_kernel(slots, counts, starts, q_ref, f_ref, *refs):
    key_refs, value_refs, refs = refs[:3], refs[3:6], refs[6:]
    shard, arrays, refs = refs[0], refs[1:7], refs[7:]
    o_ref, keys, values, ctx, acc, weight, weight_sems, sems = refs
    group = pl.program_id(0)
    groups = pl.num_programs(0)

    def output_copies():
        return weight_copies(starts, shard, arrays, 0, 1, weight, weight_sems)

    def window_copies(g):
        lanes = pl.ds(pl.multiple_of(g * WIDE, WIDE), WIDE)
        for n, (sources, target) in enumerate(((key_refs, keys), (value_refs, values))):
            for p in range(3):
                yield pltpu.make_async_copy(
                    sources[p].at[:, :, lanes],
                    target.at[g, pl.ds(p * ROWS, ROWS)],
                    sems.at[g, 3 * n + p],
                )

    @pl.when(group == 0)
    def _():
        for g in range(D // WIDE):
            for c in window_copies(g):
                c.start()
        for c in output_copies():
            c.start()

    for c in window_copies(group):
        c.wait()

    def cluster(r, carry):
        def variant(blocks):
            def run():
                head = lax.broadcasted_iota(jnp.int32, (CS, 128), 1) // HSIZE
                left = head == 0
                ids = [slots[r, j] for j in range(blocks)]
                for t in range(WIDE // 128):
                    lanes = slice(128 * t, 128 * t + 128)
                    q = q_ref[r, :, lanes]
                    stacked = jnp.concatenate(
                        [jnp.where(head == h, q, jnp.zeros_like(q)) for h in range(2)], 0
                    )
                    scores = []
                    for j in range(0, blocks, 2):
                        block = jnp.concatenate(
                            [keys[group, i, :, lanes] for i in ids[j : j + 2]], 0
                        )
                        scores.append(
                            lax.dot_general(
                                stacked,
                                block,
                                (((1,), (1,)), ((), ())),
                                preferred_element_type=F32,
                            )
                        )
                    top = None
                    for s in scores:
                        for u in range(0, s.shape[1], 128):
                            part = s[:, u : u + 128]
                            top = part if top is None else jnp.maximum(top, part)
                    top = jnp.max(top, axis=1, keepdims=True)
                    total = None
                    for n, j in enumerate(range(0, blocks, 2)):
                        probs = jnp.exp2(scores[n] - top).astype(BF)
                        vals = jnp.concatenate(
                            [values[group, i, :, lanes] for i in ids[j : j + 2]], 0
                        )
                        both = jnp.concatenate([vals, jnp.ones(vals.shape, BF)], 1)
                        d = jnp.dot(probs, both, preferred_element_type=F32)
                        total = d if total is None else total + d
                    num = jnp.where(left, total[:CS, :128], total[CS:, :128])
                    den = jnp.where(left, total[:CS, 128:], total[CS:, 128:])
                    ctx[r, :, lanes] = (num / den).astype(BF)

            return run

        lax.switch(counts[r] - 1, [variant(n) for n in range(1, 10)])
        return carry

    lax.fori_loop(0, ROWS, cluster, 0)

    @pl.when(group == 0)
    def _():
        for c in output_copies():
            c.wait()

    rows = pl.ds(pl.multiple_of(group * WIDE, WIDE), WIDE)
    part = jnp.dot(
        ctx[...].reshape(ROWS * CS, WIDE), weight[rows], preferred_element_type=F32
    )

    @pl.when(group == 0)
    def _():
        acc[...] = part

    @pl.when(jnp.logical_and(group > 0, group < groups - 1))
    def _():
        acc[...] += part

    @pl.when(group == groups - 1)
    def _():
        o_ref[...] = (f_ref[...].astype(F32) + acc[...] + part).astype(BF)


def attend(slots, counts, starts, queries, keys, values, features, shard, arrays):
    hbm = pl.BlockSpec(memory_space=pltpu.HBM)
    window = (D // WIDE, 3 * ROWS, CS, WIDE)
    return pl.pallas_call(
        attend_kernel,
        out_shape=jax.ShapeDtypeStruct((ROWS * CS, D), BF),
        grid_spec=pltpu.PrefetchScalarGridSpec(
            num_scalar_prefetch=3,
            grid=(D // WIDE,),
            in_specs=[
                pl.BlockSpec((ROWS, CS, WIDE), lambda g, *_: (0, 0, g)),
                pl.BlockSpec((ROWS * CS, D), lambda g, *_: (0, 0)),
            ]
            + [hbm] * (6 + 7),
            out_specs=pl.BlockSpec((ROWS * CS, D), lambda g, *_: (0, 0)),
            scratch_shapes=[
                pltpu.VMEM(window, BF),
                pltpu.VMEM(window, BF),
                pltpu.VMEM((ROWS, CS, WIDE), BF),
                pltpu.VMEM((ROWS * CS, D), F32),
                pltpu.VMEM((D, D), BF),
                pltpu.SemaphoreType.DMA((PIECES,)),
                pltpu.SemaphoreType.DMA((D // WIDE, 6)),
            ],
        ),
        compiler_params=pltpu.CompilerParams(vmem_limit_bytes=60 << 20),
        cost_estimate=pl.CostEstimate(
            flops=30 << 30, bytes_accessed=20 << 20, transcendentals=0
        ),
        name="attend",
    )(slots, counts, starts, queries, features, *keys, *values, shard, *arrays)


def key_slots(adjacency, valid, node, core):
    row = adjacency[:, 0, :] - node * ROWS
    low = jnp.where(core == 0, 3 * ROWS, 2 * ROWS)
    high = jnp.where(core == 0, 0, ROWS)
    index = row + jnp.where(row < 0, low, jnp.where(row >= ROWS, high, 0))
    used = (valid[:, 0, :] > 0).astype(jnp.int32)
    before = jnp.sum(
        used[:, None, :] * (jnp.arange(8)[None, :, None] > jnp.arange(8)[None, None, :]), -1
    )
    hit = used[:, :, None] * (before[:, :, None] == jnp.arange(8)[None, None, :])
    listed = jnp.sum(index[:, :, None] * hit, 1)
    own = jnp.arange(ROWS, dtype=jnp.int32)[:, None]
    return jnp.concatenate([own, listed], 1).astype(jnp.int32), (
        1 + jnp.sum(used, 1)
    ).astype(jnp.int32)


def per_device(
    features, norm_gain, query_weight, key_weight, value_weight, output_weight, adjacency, valid
):
    flat = features.reshape(ROWS * CS, D)
    n = lax.axis_size("z") * lax.axis_size("x") * 2
    pairs = [(i, i + 1) for i in range(1, n - 1, 2)]
    off = lax.ppermute(flat, NODES, pairs + [(j, i) for i, j in pairs])
    core = lax.axis_index("core")
    shards = (key_weight, value_weight, query_weight)
    part, output_part = split_rows(shards + (output_weight,), core)
    tables = (
        *key_slots(adjacency, valid, lax.axis_index(NODES), core),
        place_starts(lax.axis_index("fsdp"), core),
    )
    arrays, (slots, counts, starts) = relayed_rows(part, tables)
    output_part, _ = lax.optimization_barrier((output_part, arrays[2:4]))
    output_arrays = direct_rows(output_part)
    gain = norm_gain.reshape(1, D)
    mine, off = lax.optimization_barrier((flat, off))
    keys, values, queries = project(
        "own", mine, gain, starts, shards, arrays, 3, (1.0, 1.0, QSCALE)
    )
    near_keys, near_values = swap_cores(keys), swap_cores(values)
    queries, *output_arrays = lax.optimization_barrier((queries, *output_arrays))
    output_arrays += [swap_cores(t) for t in output_arrays]
    off_keys, off_values = project("off", off, gain, starts, shards[:2], arrays, 3, (1.0, 1.0))

    def cells(t):
        return t.reshape(ROWS, CS, D)

    out = attend(
        slots,
        counts,
        starts,
        cells(queries),
        [cells(t) for t in (keys, near_keys, off_keys)],
        [cells(t) for t in (values, near_values, off_values)],
        mine,
        output_weight,
        output_arrays,
    )
    return out.reshape(ROWS, 1, CS, D)


def solution(mesh):
    nodes, fsdp = mesh.devices.shape
    split = Mesh(mesh.devices.reshape(nodes // 8, 4, 2, fsdp), NODES + ("fsdp",))
    in_specs = (
        P(NODES, "fsdp", None, None),
        P(),
        P("fsdp", None),
        P("fsdp", None),
        P("fsdp", None),
        P("fsdp", None),
        P(NODES, "fsdp", None),
        P(NODES, "fsdp", None),
    )
    out_specs = P(NODES, "fsdp", None, None)
    return jax.shard_map(
        per_device, mesh=split, in_specs=in_specs, out_specs=out_specs, check_vma=False
    )
```

time: 155 us -> 110 us (0.71)
  the two profiles are of different devices: /device:TPU:225 before, /device:TPU:95 now
where the time goes in v2:
time: 110 us; the launch traced here: 111 us
  Pallas kernels  68.3 us (62%)
  starting transfers between devices  21.8 us (20%)
  waiting for transfers between devices  15.6 us (14%)
  local copies, waits for them, and re-layouts  3.32 us (3%)
  other arithmetic  1.63 us (1%)
    pallas_call x1, Pallas kernels, attend(): pl.pallas_call(attend_kernel, out_shape=jax.ShapeDtypeStruct((ROWS * CS,...  41.6 us
    pallas_call x2, Pallas kernels, project(): pl.pallas_call(functools.partial(project_kernel, count=count, stacked=sta...  24.4 us
    ppermute x1, waiting for transfers between devices, relayed_rows(): above = lax.ppermute(part, 'fsdp', DOWN)  10.2 us
    ppermute x9, starting transfers between devices, swap_cores(): return lax.ppermute(t, 'core', [(0, 1), (1, 0)])  6.7 us
    ppermute x1, waiting for transfers between devices, relayed_rows(): lax.ppermute(above[half:], 'fsdp', DOWN)  5.38 us
    ppermute x3, starting transfers between devices, direct_rows(): lax.ppermute(part, 'fsdp', [(i, (i + k) % 4) for i in range(4)])  5.02 us
    ppermute x1, starting transfers between devices, per_device(): off = lax.ppermute(flat, NODES, pairs + [(j, i) for i, j in pairs])  4.57 us
    ppermute x1, starting transfers between devices, relayed_rows(): lax.ppermute(below[:half], 'fsdp', UP)  2.73 us
  transfers between devices with their start and end apart: 17, of which 2 were waited for; matrix products, arithmetic and copies ran while one was open for 2% of the time, Pallas kernels for 22%

profile of v2, /device:TPU:95, one launch (start us, length us, event | category | flops | bytes accessed | tf_op | source)
XLA Modules:
  0.0 111.1 jit_solution(11464299402851561968)
XLA Ops:
  0.0 2.2 %split_rows.1 = (bf16[384,1024]{1,0:T(8,128)(2,1)}, bf16[128,1024]{1,0:T(8,128)(2,1)}) custom-call(s32[1]{0:T(128)} %bitcast.core, bf16[256,1024]{1,0:T(8,128)(2,1)} %refs_0_.3, bf16[256,1024]{1,0:T(8,128)(2,1)} %refs_1_.3, bf16[256,1024]{1,0:T(8,128)(2,1)} %refs_2_.1, bf16[256,1024]{1,0:T(8,128)(2,1)} %refs_6_.1), custom_call_target="tpu_custom_call" | custom-call | tf_op jit(solution)/shard_map/split_rows/pallas_call | solution.py:37
  2.2 0.5 collective-permute-start.1
  2.7 2.2 %collective-permute-start = (bf16[384,1024]{1,0:T(8,128)(2,1)}, bf16[384,1024]{1,0:T(8,128)(2,1)S(1)}, u32[]{:S(2)}, u32[]{:S(2)}) collective-permute-start(bf16[384,1024]{1,0:T(8,128)(2,1)} %get-tuple-element.24), channel_id=1, source_target_pairs={{0,1},{1,2},{2,3},{3,0},{4,5},{5,6},{6,7},{7,4},{8,9},{9,10},{10,1... | collective-permute-start | bytes 2359304 | tf_op jit(solution)/shard_map/ppermute | solution.py:62
  4.9 4.6 %collective-permute-start.2 = (bf16[1024,1024]{1,0:T(8,128)(2,1)}, bf16[1024,1024]{1,0:T(8,128)(2,1)}, u32[]{:S(2)}, u32[]{:S(2)}) collective-permute-start(bf16[1024,1024]{1,0:T(8,128)(2,1)} %bitcast.34), channel_id=1, source_target_pairs={{4,8},{12,16},{20,24},{28,32},{36,40},{44,48},{52,56},{60,64},{68,... | collective-permute-start | bytes 6291464 | tf_op jit(solution)/shard_map/ppermute | solution.py:345
  9.6 0.7 stack.31.starts
  10.7 0.7 pad_add_fusion.slots
  11.4 0.5 broadcast_add_fusion.counts
  11.9 10.2 %collective-permute-done.1.refs_4_.refs_3_ = bf16[384,1024]{1,0:T(8,128)(2,1)S(1)} collective-permute-done((bf16[384,1024]{1,0:T(8,128)(2,1)}, bf16[384,1024]{1,0:T(8,128)(2,1)S(1)}, u32[]{:S(2)}, u32[]{:S(2)}) %collective-permute-start.1) | collective-permute-done | bytes 786464 | tf_op jit(solution)/shard_map/ppermute | solution.py:63
  22.2 2.7 %collective-permute-start.3 = (bf16[192,1024]{1,0:T(8,128)(2,1)S(1)}, bf16[192,1024]{1,0:T(8,128)(2,1)S(1)}, u32[]{:S(2)}, u32[]{:S(2)}) collective-permute-start(bf16[192,1024]{1,0:T(8,128)(2,1)S(1)} %slice.6), channel_id=1, source_target_pairs={{0,1},{1,2},{2,3},{3,0},{4,5},{5,6},{6,7},{7,4},{8,9},{9,10},{10,1... | collective-permute-start | bytes 1179656 | tf_op jit(solution)/shard_map/ppermute | solution.py:66
  25.0 2.1 %collective-permute-start.5 = (bf16[384,1024]{1,0:T(8,128)(2,1)S(1)}, bf16[384,1024]{1,0:T(8,128)(2,1)S(1)}, u32[]{:S(2)}, u32[]{:S(2)}) collective-permute-start(bf16[384,1024]{1,0:T(8,128)(2,1)S(1)} %collective-permute-done.refs_3_.refs_2_), channel_id=1, source_target_pairs={{0,4},{4,0},{1,5},{5,1},{2,6},{6,2},{3,7},{7,3},{8,12},{12,8},{9,1... | collective-permute-start | bytes 2359304 | tf_op jit(solution)/shard_map/ppermute | solution.py:25
  27.1 5.4 %collective-permute-done.4.refs_6_.refs_5_ = bf16[192,1024]{1,0:T(8,128)(2,1)S(1)} collective-permute-done((bf16[192,1024]{1,0:T(8,128)(2,1)S(1)}, bf16[192,1024]{1,0:T(8,128)(2,1)S(1)}, u32[]{:S(2)}, u32[]{:S(2)}) %collective-permute-start.4) | collective-permute-done | bytes 393248 | tf_op jit(solution)/shard_map/ppermute | solution.py:67
  32.5 2.5 %collective-permute-start.8 = (bf16[192,1024]{1,0:T(8,128)(2,1)S(1)}, bf16[192,1024]{1,0:T(8,128)(2,1)S(1)}, u32[]{:S(2)}, u32[]{:S(2)}) collective-permute-start(bf16[192,1024]{1,0:T(8,128)(2,1)S(1)} %collective-permute-done.4.refs_6_.refs_5_), channel_id=1, source_target_pairs={{0,4},{4,0},{1,5},{5,1},{2,6},{6,2},{3,7},{7,3},{8,12},{12,8},{9,1... | collective-permute-start | bytes 1179656 | tf_op jit(solution)/shard_map/ppermute | solution.py:25
  35.0 2.3 %collective-permute-start.11 = (bf16[128,1024]{1,0:T(8,128)(2,1)}, bf16[128,1024]{1,0:T(8,128)(2,1)S(1)}, u32[]{:S(2)}, u32[]{:S(2)}) collective-permute-start(bf16[128,1024]{1,0:T(8,128)(2,1)} %get-tuple-element.33), channel_id=1, source_target_pairs={{0,2},{1,3},{2,0},{3,1},{4,6},{5,7},{6,4},{7,5},{8,10},{9,11},{10,... | collective-permute-start | bytes 786440 | tf_op jit(solution)/shard_map/ppermute | solution.py:75
  37.4 0.9 collective-permute-start.10
  38.3 1.7 %collective-permute-start.9 = (bf16[128,1024]{1,0:T(8,128)(2,1)}, bf16[128,1024]{1,0:T(8,128)(2,1)S(1)}, u32[]{:S(2)}, u32[]{:S(2)}) collective-permute-start(bf16[128,1024]{1,0:T(8,128)(2,1)} %get-tuple-element.33), channel_id=1, source_target_pairs={{0,1},{1,2},{2,3},{3,0},{4,5},{5,6},{6,7},{7,4},{8,9},{9,10},{10,1... | collective-permute-start | bytes 786440 | tf_op jit(solution)/shard_map/ppermute | solution.py:75
  40.2 0.8 copy-done.5
  41.2 13.7 %own.1 = (bf16[1024,1024]{1,0:T(8,128)(2,1)}, bf16[1024,1024]{1,0:T(8,128)(2,1)}, bf16[1024,1024]{1,0:T(8,128)(2,1)}) custom-call(s32[7]{0:T(128)} %stack.31.starts, bf16[1024,1024]{1,0:T(8,128)(2,1)} %bitcast.35, f32[1,1024]{1,0:T(1,128)} %bitcast.40, bf16[256,1024]{1,0:T(8,128)(2,1)} %refs_0_.3, bf16[256,1024]{1,0:T(8,128)(2,1)} %refs_1_.3, ...), custom_call_target="tpu_custom_call" | custom-call | flops 103079215104 | bytes 14680064 | tf_op jit(solution)/shard_map/own/pallas_call | solution.py:157
  55.0 1.0 collective-permute-start.14
  56.1 0.4 collective-permute-start.16
  56.6 0.4 collective-permute-start.13
  57.1 10.7 %off.1 = (bf16[1024,1024]{1,0:T(8,128)(2,1)}, bf16[1024,1024]{1,0:T(8,128)(2,1)}) custom-call(s32[7]{0:T(128)} %stack.31.starts, bf16[1024,1024]{1,0:T(8,128)(2,1)} %collective-permute-done.2.x_ref, f32[1,1024]{1,0:T(1,128)} %bitcast.41, bf16[256,1024]{1,0:T(8,128)(2,1)} %refs_0_.3, bf16[256,1024]{1,0:T(8,128)(2,1)} %refs_1_.3, bf16[384,1024]{1,0:T(8,128)(2,1)} %copy-done.1, ...), custom_call_target="tpu_custom_call" | custom-call | flops 68719476736 | bytes 10485760 | tf_op jit(solution)/shard_map/off/pallas_call | solution.py:157
  67.9 0.6 copy-done.14
  68.7 0.7 copy-done.4
  69.4 41.6 %attend.1 = bf16[1024,1024]{1,0:T(8,128)(2,1)} custom-call(s32[8,9]{1,0:T(8,128)} %pad_add_fusion.slots, s32[8]{0:T(128)} %broadcast_add_fusion.counts, s32[7]{0:T(128)} %stack.31.starts, bf16[8,128,1024]{2,1,0:T(8,128)(2,1)} %bitcast.42, bf16[1024,1024]{1,0:T(8,128)(2,1)} %bitcast.36, bf16[8,128,1024]{2,1,0:T(8,128)(2,1)} %bitcast.37, ...), custom_call_target="tpu_custom_call" | custom-call | flops 32212254720 | bytes 20971520 | tf_op jit(solution)/shard_map/attend/pallas_call | solution.py:292
  (60 shorter events, 1.4 us)
Async XLA Ops:
  0.0 10.2 %copy-start.2 = (s32[8,1,8]{2,1,0:T(1,128)S(1)}, s32[8,1,8]{2,1,0:T(1,128)}, u32[]{:S(2)}) copy-start(s32[8,1,8]{2,1,0:T(1,128)} %param.15) | copy-start | bytes 772
  0.0 10.6 %copy-start.3 = (s32[8,1,8]{2,1,0:T(1,128)S(1)}, s32[8,1,8]{2,1,0:T(1,128)}, u32[]{:S(2)}) copy-start(s32[8,1,8]{2,1,0:T(1,128)} %param.14) | copy-start | bytes 772
  2.2 19.8 %collective-permute-start.1 = (bf16[384,1024]{1,0:T(8,128)(2,1)}, bf16[384,1024]{1,0:T(8,128)(2,1)S(1)}, u32[]{:S(2)}, u32[]{:S(2)}) collective-permute-start(bf16[384,1024]{1,0:T(8,128)(2,1)} %get-tuple-element.24), channel_id=1, source_target_pairs={{1,0},{2,1},{3,2},{0,3},{5,4},{6,5},{7,6},{4,7},{9,8},{10,9},{11,1... | collective-permute-start | bytes 2359304 | tf_op jit(solution)/shard_map/ppermute | solution.py:63
  2.7 19.4 %collective-permute-start = (bf16[384,1024]{1,0:T(8,128)(2,1)}, bf16[384,1024]{1,0:T(8,128)(2,1)S(1)}, u32[]{:S(2)}, u32[]{:S(2)}) collective-permute-start(bf16[384,1024]{1,0:T(8,128)(2,1)} %get-tuple-element.24), channel_id=1, source_target_pairs={{0,1},{1,2},{2,3},{3,0},{4,5},{5,6},{6,7},{7,4},{8,9},{9,10},{10,1... | collective-permute-start | bytes 2359304 | tf_op jit(solution)/shard_map/ppermute | solution.py:62
  4.9 30.1 %collective-permute-start.2 = (bf16[1024,1024]{1,0:T(8,128)(2,1)}, bf16[1024,1024]{1,0:T(8,128)(2,1)}, u32[]{:S(2)}, u32[]{:S(2)}) collective-permute-start(bf16[1024,1024]{1,0:T(8,128)(2,1)} %bitcast.34), channel_id=1, source_target_pairs={{4,8},{12,16},{20,24},{28,32},{36,40},{44,48},{52,56},{60,64},{68,... | collective-permute-start | bytes 6291464 | tf_op jit(solution)/shard_map/ppermute | solution.py:345
  22.1 18.0 %copy-start = (bf16[384,1024]{1,0:T(8,128)(2,1)}, bf16[384,1024]{1,0:T(8,128)(2,1)S(1)}, u32[]{:S(2)}) copy-start(bf16[384,1024]{1,0:T(8,128)(2,1)S(1)} %collective-permute-done.1.refs_4_.refs_3_) | copy-start | bytes 2359300
  22.1 18.0 %copy-start.1 = (bf16[384,1024]{1,0:T(8,128)(2,1)}, bf16[384,1024]{1,0:T(8,128)(2,1)S(1)}, u32[]{:S(2)}) copy-start(bf16[384,1024]{1,0:T(8,128)(2,1)S(1)} %collective-permute-done.refs_3_.refs_2_) | copy-start | bytes 2359300
  22.1 10.3 %collective-permute-start.4 = (bf16[192,1024]{1,0:T(8,128)(2,1)S(1)}, bf16[192,1024]{1,0:T(8,128)(2,1)S(1)}, u32[]{:S(2)}, u32[]{:S(2)}) collective-permute-start(bf16[192,1024]{1,0:T(8,128)(2,1)S(1)} %slice.7), channel_id=1, source_target_pairs={{1,0},{2,1},{3,2},{0,3},{5,4},{6,5},{7,6},{4,7},{9,8},{10,9},{11,1... | collective-permute-start | bytes 1179656 | tf_op jit(solution)/shard_map/ppermute | solution.py:67
  22.2 12.7 %collective-permute-start.3 = (bf16[192,1024]{1,0:T(8,128)(2,1)S(1)}, bf16[192,1024]{1,0:T(8,128)(2,1)S(1)}, u32[]{:S(2)}, u32[]{:S(2)}) collective-permute-start(bf16[192,1024]{1,0:T(8,128)(2,1)S(1)} %slice.6), channel_id=1, source_target_pairs={{0,1},{1,2},{2,3},{3,0},{4,5},{5,6},{6,7},{7,4},{8,9},{9,10},{10,1... | collective-permute-start | bytes 1179656 | tf_op jit(solution)/shard_map/ppermute | solution.py:66
  25.0 15.1 %collective-permute-start.5 = (bf16[384,1024]{1,0:T(8,128)(2,1)S(1)}, bf16[384,1024]{1,0:T(8,128)(2,1)S(1)}, u32[]{:S(2)}, u32[]{:S(2)}) collective-permute-start(bf16[384,1024]{1,0:T(8,128)(2,1)S(1)} %collective-permute-done.refs_3_.refs_2_), channel_id=1, source_target_pairs={{0,4},{4,0},{1,5},{5,1},{2,6},{6,2},{3,7},{7,3},{8,12},{12,8},{9,1... | collective-permute-start | bytes 2359304 | tf_op jit(solution)/shard_map/ppermute | solution.py:25
  27.1 13.0 %collective-permute-start.6 = (bf16[384,1024]{1,0:T(8,128)(2,1)S(1)}, bf16[384,1024]{1,0:T(8,128)(2,1)S(1)}, u32[]{:S(2)}, u32[]{:S(2)}) collective-permute-start(bf16[384,1024]{1,0:T(8,128)(2,1)S(1)} %collective-permute-done.1.refs_4_.refs_3_), channel_id=1, source_target_pairs={{0,4},{4,0},{1,5},{5,1},{2,6},{6,2},{3,7},{7,3},{8,12},{12,8},{9,1... | collective-permute-start | bytes 2359304 | tf_op jit(solution)/shard_map/ppermute | solution.py:25
  32.5 4.9 %collective-permute-start.8 = (bf16[192,1024]{1,0:T(8,128)(2,1)S(1)}, bf16[192,1024]{1,0:T(8,128)(2,1)S(1)}, u32[]{:S(2)}, u32[]{:S(2)}) collective-permute-start(bf16[192,1024]{1,0:T(8,128)(2,1)S(1)} %collective-permute-done.4.refs_6_.refs_5_), channel_id=1, source_target_pairs={{0,4},{4,0},{1,5},{5,1},{2,6},{6,2},{3,7},{7,3},{8,12},{12,8},{9,1... | collective-permute-start | bytes 1179656 | tf_op jit(solution)/shard_map/ppermute | solution.py:25
  34.9 3.4 %collective-permute-start.7 = (bf16[192,1024]{1,0:T(8,128)(2,1)S(1)}, bf16[192,1024]{1,0:T(8,128)(2,1)S(1)}, u32[]{:S(2)}, u32[]{:S(2)}) collective-permute-start(bf16[192,1024]{1,0:T(8,128)(2,1)S(1)} %collective-permute-done.3.refs_5_.refs_4_), channel_id=1, source_target_pairs={{0,4},{4,0},{1,5},{5,1},{2,6},{6,2},{3,7},{7,3},{8,12},{12,8},{9,1... | collective-permute-start | bytes 1179656 | tf_op jit(solution)/shard_map/ppermute | solution.py:25
  35.0 19.9 %collective-permute-start.11 = (bf16[128,1024]{1,0:T(8,128)(2,1)}, bf16[128,1024]{1,0:T(8,128)(2,1)S(1)}, u32[]{:S(2)}, u32[]{:S(2)}) collective-permute-start(bf16[128,1024]{1,0:T(8,128)(2,1)} %get-tuple-element.33), channel_id=1, source_target_pairs={{0,2},{1,3},{2,0},{3,1},{4,6},{5,7},{6,4},{7,5},{8,10},{9,11},{10,... | collective-permute-start | bytes 786440 | tf_op jit(solution)/shard_map/ppermute | solution.py:75
  37.4 17.6 %collective-permute-start.10 = (bf16[128,1024]{1,0:T(8,128)(2,1)}, bf16[128,1024]{1,0:T(8,128)(2,1)S(1)}, u32[]{:S(2)}, u32[]{:S(2)}) collective-permute-start(bf16[128,1024]{1,0:T(8,128)(2,1)} %get-tuple-element.33), channel_id=1, source_target_pairs={{0,3},{1,0},{2,1},{3,2},{4,7},{5,4},{6,5},{7,6},{8,11},{9,8},{10,9... | collective-permute-start | bytes 786440 | tf_op jit(solution)/shard_map/ppermute | solution.py:75
  38.3 16.7 %collective-permute-start.9 = (bf16[128,1024]{1,0:T(8,128)(2,1)}, bf16[128,1024]{1,0:T(8,128)(2,1)S(1)}, u32[]{:S(2)}, u32[]{:S(2)}) collective-permute-start(bf16[128,1024]{1,0:T(8,128)(2,1)} %get-tuple-element.33), channel_id=1, source_target_pairs={{0,1},{1,2},{2,3},{3,0},{4,5},{5,6},{6,7},{7,4},{8,9},{9,10},{10,1... | collective-permute-start | bytes 786440 | tf_op jit(solution)/shard_map/ppermute | solution.py:75
  55.0 12.8 %copy-start.11 = (bf16[128,1024]{1,0:T(8,128)(2,1)}, bf16[128,1024]{1,0:T(8,128)(2,1)S(1)}, u32[]{:S(2)}) copy-start(bf16[128,1024]{1,0:T(8,128)(2,1)S(1)} %collective-permute-done.11.refs_9_) | copy-start | bytes 786436
  55.0 12.8 %copy-start.12 = (bf16[128,1024]{1,0:T(8,128)(2,1)}, bf16[128,1024]{1,0:T(8,128)(2,1)S(1)}, u32[]{:S(2)}) copy-start(bf16[128,1024]{1,0:T(8,128)(2,1)S(1)} %collective-permute-done.10.refs_8_) | copy-start | bytes 786436
  55.0 12.8 %copy-start.13 = (bf16[128,1024]{1,0:T(8,128)(2,1)}, bf16[128,1024]{1,0:T(8,128)(2,1)S(1)}, u32[]{:S(2)}) copy-start(bf16[128,1024]{1,0:T(8,128)(2,1)S(1)} %collective-permute-done.9.refs_7_) | copy-start | bytes 786436
  55.0 12.8 %collective-permute-start.14 = (bf16[128,1024]{1,0:T(8,128)(2,1)S(1)}, bf16[128,1024]{1,0:T(8,128)(2,1)S(1)}, u32[]{:S(2)}, u32[]{:S(2)}) collective-permute-start(bf16[128,1024]{1,0:T(8,128)(2,1)S(1)} %collective-permute-done.9.refs_7_), channel_id=1, source_target_pairs={{0,4},{4,0},{1,5},{5,1},{2,6},{6,2},{3,7},{7,3},{8,12},{12,8},{9,1... | collective-permute-start | bytes 786440 | tf_op jit(solution)/shard_map/ppermute | solution.py:25
  56.0 11.8 %collective-permute-start.15 = (bf16[128,1024]{1,0:T(8,128)(2,1)S(1)}, bf16[128,1024]{1,0:T(8,128)(2,1)S(1)}, u32[]{:S(2)}, u32[]{:S(2)}) collective-permute-start(bf16[128,1024]{1,0:T(8,128)(2,1)S(1)} %collective-permute-done.10.refs_8_), channel_id=1, source_target_pairs={{0,4},{4,0},{1,5},{5,1},{2,6},{6,2},{3,7},{7,3},{8,12},{12,8},{9,1... | collective-permute-start | bytes 786440 | tf_op jit(solution)/shard_map/ppermute | solution.py:25
  56.1 11.7 %collective-permute-start.16 = (bf16[128,1024]{1,0:T(8,128)(2,1)S(1)}, bf16[128,1024]{1,0:T(8,128)(2,1)S(1)}, u32[]{:S(2)}, u32[]{:S(2)}) collective-permute-start(bf16[128,1024]{1,0:T(8,128)(2,1)S(1)} %collective-permute-done.11.refs_9_), channel_id=1, source_target_pairs={{0,4},{4,0},{1,5},{5,1},{2,6},{6,2},{3,7},{7,3},{8,12},{12,8},{9,1... | collective-permute-start | bytes 786440 | tf_op jit(solution)/shard_map/ppermute | solution.py:25
  56.5 11.3 %collective-permute-start.12 = (bf16[1024,1024]{1,0:T(8,128)(2,1)}, bf16[1024,1024]{1,0:T(8,128)(2,1)S(1)}, u32[]{:S(2)}, u32[]{:S(2)}) collective-permute-start(bf16[1024,1024]{1,0:T(8,128)(2,1)} %get-tuple-element.35), channel_id=1, source_target_pairs={{0,4},{4,0},{1,5},{5,1},{2,6},{6,2},{3,7},{7,3},{8,12},{12,8},{9,1... | collective-permute-start | bytes 6291464 | tf_op jit(solution)/shard_map/ppermute | solution.py:25
  56.6 11.2 %collective-permute-start.13 = (bf16[1024,1024]{1,0:T(8,128)(2,1)}, bf16[1024,1024]{1,0:T(8,128)(2,1)}, u32[]{:S(2)}, u32[]{:S(2)}) collective-permute-start(bf16[1024,1024]{1,0:T(8,128)(2,1)} %get-tuple-element.38), channel_id=1, source_target_pairs={{0,4},{4,0},{1,5},{5,1},{2,6},{6,2},{3,7},{7,3},{8,12},{12,8},{9,1... | collective-permute-start | bytes 6291464 | tf_op jit(solution)/shard_map/ppermute | solution.py:25
  (10 other events, 23.3 us)

commit v3 on v2

--- a/solution.py
+++ b/solution.py
@@ -19,6 +19,7 @@
 TILE = 256
 SHARD = 256
 WIDE = 512
+SAFE = 9000.0
 
 
 def swap_cores(t):
@@ -121,9 +122,19 @@
 PIECES = 9
 
 
-def project_kernel(starts, x_ref, gain_ref, *refs, count, stacked, scales):
+def head_squares(t):
+    wide = D // 2
+    squares = t[:, :wide] * t[:, :wide] + t[:, wide:] * t[:, wide:]
+    lane = lax.broadcasted_iota(jnp.int32, (wide, 128), 1)
+    feature = lax.broadcasted_iota(jnp.int32, (wide, 128), 0)
+    pick = (feature // HSIZE == lane).astype(BF)
+    sums = jnp.dot(squares.astype(BF), pick, preferred_element_type=F32)
+    return jnp.broadcast_to(jnp.max(sums, axis=0, keepdims=True), (8, 128))
+
+
+def project_kernel(starts, x_ref, gain_ref, *refs, count, stacked, scales, squared):
     shards, arrays, refs = refs[:count], refs[count : count + 8], refs[count + 8 :]
-    outs, (weights, sems) = refs[:count], refs[count:]
+    outs, squares, (weights, sems) = refs[:count], refs[count:-2], refs[-2:]
     step = pl.program_id(0)
 
     def copies(w):
@@ -134,6 +145,8 @@
         for w in range(count):
             for c in copies(w):
                 c.start()
+        for ref in squares:
+            ref[...] = jnp.zeros_like(ref)
 
     wide = x_ref[...].astype(F32)
     mean = jnp.mean(wide * wide, axis=-1, keepdims=True)
@@ -148,15 +161,21 @@
         got = jnp.dot(normed, weights[w], preferred_element_type=F32)
         if scales[w] != 1.0:
             got = got * scales[w]
+        if w in squared:
+            ref = squares[squared.index(w)]
+            ref[...] = jnp.maximum(ref[...], head_squares(got))
         outs[w][...] = got.astype(BF)
 
 
-def project(name, x, gain, starts, shards, arrays, stacked, scales):
+def project(name, x, gain, starts, shards, arrays, stacked, scales, squared):
     count = len(shards)
     rows = x.shape[0]
     return pl.pallas_call(
-        functools.partial(project_kernel, count=count, stacked=stacked, scales=scales),
-        out_shape=[jax.ShapeDtypeStruct((rows, D), BF)] * count,
+        functools.partial(
+            project_kernel, count=count, stacked=stacked, scales=scales, squared=squared
+        ),
+        out_shape=[jax.ShapeDtypeStruct((rows, D), BF)] * count
+        + [jax.ShapeDtypeStruct((8, 128), F32)] * len(squared),
         grid_spec=pltpu.PrefetchScalarGridSpec(
             num_scalar_prefetch=1,
             grid=(rows // TILE,),
@@ -165,7 +184,8 @@
                 pl.BlockSpec((1, D), lambda i, s: (0, 0)),
             ]
             + [pl.BlockSpec(memory_space=pltpu.HBM)] * (count + 8),
-            out_specs=[pl.BlockSpec((TILE, D), lambda i, s: (i, 0))] * count,
+            out_specs=[pl.BlockSpec((TILE, D), lambda i, s: (i, 0))] * count
+            + [pl.BlockSpec((8, 128), lambda i, s: (0, 0))] * len(squared),
             scratch_shapes=[
                 pltpu.VMEM((count, D, D), BF),
                 pltpu.SemaphoreType.DMA((count, PIECES)),
@@ -182,6 +202,7 @@
 
 
 def attend_kernel(slots, counts, starts, q_ref, f_ref, *refs):
+    square_refs, refs = refs[:4], refs[4:]
     key_refs, value_refs, refs = refs[:3], refs[3:6], refs[6:]
     shard, arrays, refs = refs[0], refs[1:7], refs[7:]
     o_ref, keys, values, ctx, acc, weight, weight_sems, sems = refs
@@ -212,8 +233,13 @@
     for c in window_copies(group):
         c.wait()
 
+    key_squares = jnp.maximum(
+        jnp.maximum(square_refs[0][...], square_refs[1][...]), square_refs[2][...]
+    )
+    shifted = jnp.where(jnp.max(key_squares * square_refs[3][...]) < SAFE, 0, 9)
+
     def cluster(r, carry):
-        def variant(blocks):
+        def variant(blocks, shift):
             def run():
                 head = lax.broadcasted_iota(jnp.int32, (CS, 128), 1) // HSIZE
                 left = head == 0
@@ -237,15 +263,17 @@
                                 preferred_element_type=F32,
                             )
                         )
-                    top = None
-                    for s in scores:
-                        for u in range(0, s.shape[1], 128):
-                            part = s[:, u : u + 128]
-                            top = part if top is None else jnp.maximum(top, part)
-                    top = jnp.max(top, axis=1, keepdims=True)
+                    if shift:
+                        top = None
+                        for s in scores:
+                            for u in range(0, s.shape[1], 128):
+                                part = s[:, u : u + 128]
+                                top = part if top is None else jnp.maximum(top, part)
+                        top = jnp.max(top, axis=1, keepdims=True)
+                        scores = [s - top for s in scores]
                     total = None
                     for n, j in enumerate(range(0, blocks, 2)):
-                        probs = jnp.exp2(scores[n] - top).astype(BF)
+                        probs = jnp.exp2(scores[n]).astype(BF)
                         vals = jnp.concatenate(
                             [values[group, i, :, lanes] for i in ids[j : j + 2]], 0
                         )
@@ -258,7 +286,10 @@
 
             return run
 
-        lax.switch(counts[r] - 1, [variant(n) for n in range(1, 10)])
+        lax.switch(
+            counts[r] - 1 + shifted,
+            [variant(n, shift) for shift in (False, True) for n in range(1, 10)],
+        )
         return carry
 
     lax.fori_loop(0, ROWS, cluster, 0)
@@ -286,7 +317,7 @@
         o_ref[...] = (f_ref[...].astype(F32) + acc[...] + part).astype(BF)
 
 
-def attend(slots, counts, starts, queries, keys, values, features, shard, arrays):
+def attend(slots, counts, starts, queries, keys, values, squares, features, shard, arrays):
     hbm = pl.BlockSpec(memory_space=pltpu.HBM)
     window = (D // WIDE, 3 * ROWS, CS, WIDE)
     return pl.pallas_call(
@@ -299,6 +330,7 @@
                 pl.BlockSpec((ROWS, CS, WIDE), lambda g, *_: (0, 0, g)),
                 pl.BlockSpec((ROWS * CS, D), lambda g, *_: (0, 0)),
             ]
+            + [pl.BlockSpec((8, 128), lambda g, *_: (0, 0))] * 4
             + [hbm] * (6 + 7),
             out_specs=pl.BlockSpec((ROWS * CS, D), lambda g, *_: (0, 0)),
             scratch_shapes=[
@@ -316,7 +348,7 @@
             flops=30 << 30, bytes_accessed=20 << 20, transcendentals=0
         ),
         name="attend",
-    )(slots, counts, starts, queries, features, *keys, *values, shard, *arrays)
+    )(slots, counts, starts, queries, features, *squares, *keys, *values, shard, *arrays)
 
 
 def key_slots(adjacency, valid, node, core):
@@ -355,13 +387,16 @@
     output_arrays = direct_rows(output_part)
     gain = norm_gain.reshape(1, D)
     mine, off = lax.optimization_barrier((flat, off))
-    keys, values, queries = project(
-        "own", mine, gain, starts, shards, arrays, 3, (1.0, 1.0, QSCALE)
+    keys, values, queries, own_squares, query_squares = project(
+        "own", mine, gain, starts, shards, arrays, 3, (1.0, 1.0, QSCALE), (0, 2)
     )
     near_keys, near_values = swap_cores(keys), swap_cores(values)
+    near_squares = swap_cores(own_squares)
     queries, *output_arrays = lax.optimization_barrier((queries, *output_arrays))
     output_arrays += [swap_cores(t) for t in output_arrays]
-    off_keys, off_values = project("off", off, gain, starts, shards[:2], arrays, 3, (1.0, 1.0))
+    off_keys, off_values, off_squares = project(
+        "off", off, gain, starts, shards[:2], arrays, 3, (1.0, 1.0), (0,)
+    )
 
     def cells(t):
         return t.reshape(ROWS, CS, D)
@@ -373,6 +408,7 @@
         cells(queries),
         [cells(t) for t in (keys, near_keys, off_keys)],
         [cells(t) for t in (values, near_values, off_values)],
+        (own_squares, near_squares, off_squares, query_squares),
         mine,
         output_weight,
         output_arrays,

time: 110 us -> 114 us (1.036)
  the two profiles are of different devices: /device:TPU:95 before, /device:TPU:103 now
where the time goes in v3:
time: 114 us; the launch traced here: 112 us
  Pallas kernels  68.7 us (60%)
  starting transfers between devices  21.1 us (19%)
  waiting for transfers between devices  16.5 us (14%)
  local copies, waits for them, and re-layouts  3.34 us (3%)
  other arithmetic  1.61 us (1%)
    pallas_call x1, Pallas kernels, attend(): pl.pallas_call(attend_kernel, out_shape=jax.ShapeDtypeStruct((ROWS * CS,...  40.2 us
    pallas_call x2, Pallas kernels, project(): pl.pallas_call(functools.partial(project_kernel, count=count, stacked=sta...  26.2 us
    ppermute x10, starting transfers between devices, swap_cores(): return lax.ppermute(t, 'core', [(0, 1), (1, 0)])  8.91 us
    ppermute x1, waiting for transfers between devices, relayed_rows(): above = lax.ppermute(part, 'fsdp', DOWN)  8.73 us
    ppermute x1, starting transfers between devices, per_device(): off = lax.ppermute(flat, NODES, pairs + [(j, i) for i, j in pairs])  5.5 us
    ppermute x1, waiting for transfers between devices, relayed_rows(): lax.ppermute(above[half:], 'fsdp', DOWN)  4.74 us
    ppermute x1, waiting for transfers between devices, relayed_rows(): below = lax.ppermute(part, 'fsdp', UP)  2.99 us
    ppermute x1, starting transfers between devices, relayed_rows(): above = lax.ppermute(part, 'fsdp', DOWN)  2.73 us
  transfers between devices with their start and end apart: 18, of which 3 were waited for; matrix products, arithmetic and copies ran while one was open for 2% of the time, Pallas kernels for 23%

profile of v3, /device:TPU:103, one launch (start us, length us, event | category | flops | bytes accessed | tf_op | source)
XLA Modules:
  0.0 111.8 jit_solution(16292011075189172057)
XLA Ops:
  0.0 2.2 %split_rows.1 = (bf16[384,1024]{1,0:T(8,128)(2,1)}, bf16[128,1024]{1,0:T(8,128)(2,1)}) custom-call(s32[1]{0:T(128)} %bitcast.core, bf16[256,1024]{1,0:T(8,128)(2,1)} %refs_0_.3, bf16[256,1024]{1,0:T(8,128)(2,1)} %refs_1_.3, bf16[256,1024]{1,0:T(8,128)(2,1)} %refs_2_.1, bf16[256,1024]{1,0:T(8,128)(2,1)} %refs_10_.1), custom_call_target="tpu_custom_call" | custom-call | tf_op jit(solution)/shard_map/split_rows/pallas_call | solution.py:38
  2.3 2.7 %collective-permute-start.1 = (bf16[384,1024]{1,0:T(8,128)(2,1)}, bf16[384,1024]{1,0:T(8,128)(2,1)S(1)}, u32[]{:S(2)}, u32[]{:S(2)}) collective-permute-start(bf16[384,1024]{1,0:T(8,128)(2,1)} %get-tuple-element.27), channel_id=1, source_target_pairs={{1,0},{2,1},{3,2},{0,3},{5,4},{6,5},{7,6},{4,7},{9,8},{10,9},{11,1... | collective-permute-start | bytes 2359304 | tf_op jit(solution)/shard_map/ppermute | solution.py:64
  5.0 5.5 %collective-permute-start.2 = (bf16[1024,1024]{1,0:T(8,128)(2,1)}, bf16[1024,1024]{1,0:T(8,128)(2,1)}, u32[]{:S(2)}, u32[]{:S(2)}) collective-permute-start(bf16[1024,1024]{1,0:T(8,128)(2,1)} %bitcast.34), channel_id=1, source_target_pairs={{4,8},{12,16},{20,24},{28,32},{36,40},{44,48},{52,56},{60,64},{68,... | collective-permute-start | bytes 6291464 | tf_op jit(solution)/shard_map/ppermute | solution.py:377
  10.6 0.6 stack.31.starts
  11.6 0.7 pad_add_fusion.slots
  12.3 0.5 broadcast_add_fusion.counts
  12.8 8.7 %collective-permute-done.1.refs_4_.refs_3_ = bf16[384,1024]{1,0:T(8,128)(2,1)S(1)} collective-permute-done((bf16[384,1024]{1,0:T(8,128)(2,1)}, bf16[384,1024]{1,0:T(8,128)(2,1)S(1)}, u32[]{:S(2)}, u32[]{:S(2)}) %collective-permute-start.1) | collective-permute-done | bytes 786464 | tf_op jit(solution)/shard_map/ppermute | solution.py:64
  21.5 3.0 %collective-permute-done.refs_3_.refs_2_ = bf16[384,1024]{1,0:T(8,128)(2,1)S(1)} collective-permute-done((bf16[384,1024]{1,0:T(8,128)(2,1)}, bf16[384,1024]{1,0:T(8,128)(2,1)S(1)}, u32[]{:S(2)}, u32[]{:S(2)}) %collective-permute-start) | collective-permute-done | bytes 786464 | tf_op jit(solution)/shard_map/ppermute | solution.py:63
  24.5 0.4 collective-permute-start.4
  25.0 1.2 %collective-permute-start.3 = (bf16[192,1024]{1,0:T(8,128)(2,1)S(1)}, bf16[192,1024]{1,0:T(8,128)(2,1)S(1)}, u32[]{:S(2)}, u32[]{:S(2)}) collective-permute-start(bf16[192,1024]{1,0:T(8,128)(2,1)S(1)} %slice.6), channel_id=1, source_target_pairs={{0,1},{1,2},{2,3},{3,0},{4,5},{5,6},{6,7},{7,4},{8,9},{9,10},{10,1... | collective-permute-start | bytes 1179656 | tf_op jit(solution)/shard_map/ppermute | solution.py:67
  26.2 2.4 %collective-permute-start.5 = (bf16[384,1024]{1,0:T(8,128)(2,1)S(1)}, bf16[384,1024]{1,0:T(8,128)(2,1)S(1)}, u32[]{:S(2)}, u32[]{:S(2)}) collective-permute-start(bf16[384,1024]{1,0:T(8,128)(2,1)S(1)} %collective-permute-done.refs_3_.refs_2_), channel_id=1, source_target_pairs={{0,4},{4,0},{1,5},{5,1},{2,6},{6,2},{3,7},{7,3},{8,12},{12,8},{9,1... | collective-permute-start | bytes 2359304 | tf_op jit(solution)/shard_map/ppermute | solution.py:26
  28.6 4.7 %collective-permute-done.4.refs_6_.refs_5_ = bf16[192,1024]{1,0:T(8,128)(2,1)S(1)} collective-permute-done((bf16[192,1024]{1,0:T(8,128)(2,1)S(1)}, bf16[192,1024]{1,0:T(8,128)(2,1)S(1)}, u32[]{:S(2)}, u32[]{:S(2)}) %collective-permute-start.4) | collective-permute-done | bytes 393248 | tf_op jit(solution)/shard_map/ppermute | solution.py:68
  33.4 2.8 %collective-permute-start.8 = (bf16[192,1024]{1,0:T(8,128)(2,1)S(1)}, bf16[192,1024]{1,0:T(8,128)(2,1)S(1)}, u32[]{:S(2)}, u32[]{:S(2)}) collective-permute-start(bf16[192,1024]{1,0:T(8,128)(2,1)S(1)} %collective-permute-done.4.refs_6_.refs_5_), channel_id=1, source_target_pairs={{0,4},{4,0},{1,5},{5,1},{2,6},{6,2},{3,7},{7,3},{8,12},{12,8},{9,1... | collective-permute-start | bytes 1179656 | tf_op jit(solution)/shard_map/ppermute | solution.py:26
  36.1 1.6 %collective-permute-start.7 = (bf16[192,1024]{1,0:T(8,128)(2,1)S(1)}, bf16[192,1024]{1,0:T(8,128)(2,1)S(1)}, u32[]{:S(2)}, u32[]{:S(2)}) collective-permute-start(bf16[192,1024]{1,0:T(8,128)(2,1)S(1)} %collective-permute-done.3.refs_5_.refs_4_), channel_id=1, source_target_pairs={{0,4},{4,0},{1,5},{5,1},{2,6},{6,2},{3,7},{7,3},{8,12},{12,8},{9,1... | collective-permute-start | bytes 1179656 | tf_op jit(solution)/shard_map/ppermute | solution.py:26
  38.1 2.1 %collective-permute-start.10 = (bf16[128,1024]{1,0:T(8,128)(2,1)}, bf16[128,1024]{1,0:T(8,128)(2,1)S(1)}, u32[]{:S(2)}, u32[]{:S(2)}) collective-permute-start(bf16[128,1024]{1,0:T(8,128)(2,1)} %get-tuple-element.36), channel_id=1, source_target_pairs={{0,3},{1,0},{2,1},{3,2},{4,7},{5,4},{6,5},{7,6},{8,11},{9,8},{10,9... | collective-permute-start | bytes 786440 | tf_op jit(solution)/shard_map/ppermute | solution.py:76
  40.2 0.7 copy-done.10
  41.4 14.9 %own.1 = (bf16[1024,1024]{1,0:T(8,128)(2,1)}, bf16[1024,1024]{1,0:T(8,128)(2,1)}, bf16[1024,1024]{1,0:T(8,128)(2,1)}, f32[8,128]{1,0:T(8,128)}, f32[8,128]{1,0:T(8,128)}) custom-call(s32[7]{0:T(128)} %stack.31.starts, bf16[1024,1024]{1,0:T(8,128)(2,1)} %bitcast.35, f32[1,1024]{1,0:T(1,128)} %bitcast.40, bf16[256,1024]{1,0:T(8,128)(2,1)} %refs_0_.3, ...), custom_call_target="tpu_custom_call" | custom-call | flops 103079215104 | bytes 14680064 | tf_op jit(solution)/shard_map/own/pallas_call | solution.py:173
  56.3 0.7 collective-permute-start.12
  57.1 0.5 collective-permute-start.16
  57.7 0.4 collective-permute-start.13
  58.4 11.4 %off.1 = (bf16[1024,1024]{1,0:T(8,128)(2,1)}, bf16[1024,1024]{1,0:T(8,128)(2,1)}, f32[8,128]{1,0:T(8,128)}) custom-call(s32[7]{0:T(128)} %stack.31.starts, bf16[1024,1024]{1,0:T(8,128)(2,1)} %collective-permute-done.2.x_ref, f32[1,1024]{1,0:T(1,128)} %bitcast.41, bf16[256,1024]{1,0:T(8,128)(2,1)} %refs_0_.3, bf16[256,1024]{1,0:T(8,128)(2,1)} %refs_1_.3, ...), custom_call_target="tpu_custom_call" | custom-call | flops 68719476736 | bytes 10485760 | tf_op jit(solution)/shard_map/off/pallas_call | solution.py:173
  69.9 0.6 copy-done.14
  70.7 0.7 copy-done.4
  71.4 40.2 %attend.1 = bf16[1024,1024]{1,0:T(8,128)(2,1)} custom-call(s32[8,9]{1,0:T(8,128)} %pad_add_fusion.slots, s32[8]{0:T(128)} %broadcast_add_fusion.counts, s32[7]{0:T(128)} %stack.31.starts, bf16[8,128,1024]{2,1,0:T(8,128)(2,1)} %bitcast.42, bf16[1024,1024]{1,0:T(8,128)(2,1)} %bitcast.36, f32[8,128]{1,0:T(8,128)} %get-tuple-element.38.refs_0_, ...), custom_call_target="tpu_custom_call" | custom-call | flops 32212254720 | bytes 20971520 | tf_op jit(solution)/shard_map/attend/pallas_call | solution.py:323
  (64 shorter events, 2.0 us)
Async XLA Ops:
  2.3 19.3 %collective-permute-start.1 = (bf16[384,1024]{1,0:T(8,128)(2,1)}, bf16[384,1024]{1,0:T(8,128)(2,1)S(1)}, u32[]{:S(2)}, u32[]{:S(2)}) collective-permute-start(bf16[384,1024]{1,0:T(8,128)(2,1)} %get-tuple-element.27), channel_id=1, source_target_pairs={{1,0},{2,1},{3,2},{0,3},{5,4},{6,5},{7,6},{4,7},{9,8},{10,9},{11,1... | collective-permute-start | bytes 2359304 | tf_op jit(solution)/shard_map/ppermute | solution.py:64
  5.0 19.5 %collective-permute-start = (bf16[384,1024]{1,0:T(8,128)(2,1)}, bf16[384,1024]{1,0:T(8,128)(2,1)S(1)}, u32[]{:S(2)}, u32[]{:S(2)}) collective-permute-start(bf16[384,1024]{1,0:T(8,128)(2,1)} %get-tuple-element.27), channel_id=1, source_target_pairs={{0,1},{1,2},{2,3},{3,0},{4,5},{5,6},{6,7},{7,4},{8,9},{9,10},{10,1... | collective-permute-start | bytes 2359304 | tf_op jit(solution)/shard_map/ppermute | solution.py:63
  5.0 32.8 %collective-permute-start.2 = (bf16[1024,1024]{1,0:T(8,128)(2,1)}, bf16[1024,1024]{1,0:T(8,128)(2,1)}, u32[]{:S(2)}, u32[]{:S(2)}) collective-permute-start(bf16[1024,1024]{1,0:T(8,128)(2,1)} %bitcast.34), channel_id=1, source_target_pairs={{4,8},{12,16},{20,24},{28,32},{36,40},{44,48},{52,56},{60,64},{68,... | collective-permute-start | bytes 6291464 | tf_op jit(solution)/shard_map/ppermute | solution.py:377
  21.5 18.7 %copy-start = (bf16[384,1024]{1,0:T(8,128)(2,1)}, bf16[384,1024]{1,0:T(8,128)(2,1)S(1)}, u32[]{:S(2)}) copy-start(bf16[384,1024]{1,0:T(8,128)(2,1)S(1)} %collective-permute-done.1.refs_4_.refs_3_) | copy-start | bytes 2359300
  24.5 15.7 %copy-start.1 = (bf16[384,1024]{1,0:T(8,128)(2,1)}, bf16[384,1024]{1,0:T(8,128)(2,1)S(1)}, u32[]{:S(2)}) copy-start(bf16[384,1024]{1,0:T(8,128)(2,1)S(1)} %collective-permute-done.refs_3_.refs_2_) | copy-start | bytes 2359300
  24.5 8.8 %collective-permute-start.4 = (bf16[192,1024]{1,0:T(8,128)(2,1)S(1)}, bf16[192,1024]{1,0:T(8,128)(2,1)S(1)}, u32[]{:S(2)}, u32[]{:S(2)}) collective-permute-start(bf16[192,1024]{1,0:T(8,128)(2,1)S(1)} %slice.7), channel_id=1, source_target_pairs={{1,0},{2,1},{3,2},{0,3},{5,4},{6,5},{7,6},{4,7},{9,8},{10,9},{11,1... | collective-permute-start | bytes 1179656 | tf_op jit(solution)/shard_map/ppermute | solution.py:68
  25.0 11.2 %collective-permute-start.3 = (bf16[192,1024]{1,0:T(8,128)(2,1)S(1)}, bf16[192,1024]{1,0:T(8,128)(2,1)S(1)}, u32[]{:S(2)}, u32[]{:S(2)}) collective-permute-start(bf16[192,1024]{1,0:T(8,128)(2,1)S(1)} %slice.6), channel_id=1, source_target_pairs={{0,1},{1,2},{2,3},{3,0},{4,5},{5,6},{6,7},{7,4},{8,9},{9,10},{10,1... | collective-permute-start | bytes 1179656 | tf_op jit(solution)/shard_map/ppermute | solution.py:67
  26.2 14.0 %collective-permute-start.5 = (bf16[384,1024]{1,0:T(8,128)(2,1)S(1)}, bf16[384,1024]{1,0:T(8,128)(2,1)S(1)}, u32[]{:S(2)}, u32[]{:S(2)}) collective-permute-start(bf16[384,1024]{1,0:T(8,128)(2,1)S(1)} %collective-permute-done.refs_3_.refs_2_), channel_id=1, source_target_pairs={{0,4},{4,0},{1,5},{5,1},{2,6},{6,2},{3,7},{7,3},{8,12},{12,8},{9,1... | collective-permute-start | bytes 2359304 | tf_op jit(solution)/shard_map/ppermute | solution.py:26
  28.6 11.6 %collective-permute-start.6 = (bf16[384,1024]{1,0:T(8,128)(2,1)S(1)}, bf16[384,1024]{1,0:T(8,128)(2,1)S(1)}, u32[]{:S(2)}, u32[]{:S(2)}) collective-permute-start(bf16[384,1024]{1,0:T(8,128)(2,1)S(1)} %collective-permute-done.1.refs_4_.refs_3_), channel_id=1, source_target_pairs={{0,4},{4,0},{1,5},{5,1},{2,6},{6,2},{3,7},{7,3},{8,12},{12,8},{9,1... | collective-permute-start | bytes 2359304 | tf_op jit(solution)/shard_map/ppermute | solution.py:26
  33.4 4.7 %collective-permute-start.8 = (bf16[192,1024]{1,0:T(8,128)(2,1)S(1)}, bf16[192,1024]{1,0:T(8,128)(2,1)S(1)}, u32[]{:S(2)}, u32[]{:S(2)}) collective-permute-start(bf16[192,1024]{1,0:T(8,128)(2,1)S(1)} %collective-permute-done.4.refs_6_.refs_5_), channel_id=1, source_target_pairs={{0,4},{4,0},{1,5},{5,1},{2,6},{6,2},{3,7},{7,3},{8,12},{12,8},{9,1... | collective-permute-start | bytes 1179656 | tf_op jit(solution)/shard_map/ppermute | solution.py:26
  36.1 4.0 %collective-permute-start.7 = (bf16[192,1024]{1,0:T(8,128)(2,1)S(1)}, bf16[192,1024]{1,0:T(8,128)(2,1)S(1)}, u32[]{:S(2)}, u32[]{:S(2)}) collective-permute-start(bf16[192,1024]{1,0:T(8,128)(2,1)S(1)} %collective-permute-done.3.refs_5_.refs_4_), channel_id=1, source_target_pairs={{0,4},{4,0},{1,5},{5,1},{2,6},{6,2},{3,7},{7,3},{8,12},{12,8},{9,1... | collective-permute-start | bytes 1179656 | tf_op jit(solution)/shard_map/ppermute | solution.py:26
  37.8 19.2 %collective-permute-start.11 = (bf16[128,1024]{1,0:T(8,128)(2,1)}, bf16[128,1024]{1,0:T(8,128)(2,1)S(1)}, u32[]{:S(2)}, u32[]{:S(2)}) collective-permute-start(bf16[128,1024]{1,0:T(8,128)(2,1)} %get-tuple-element.36), channel_id=1, source_target_pairs={{0,2},{1,3},{2,0},{3,1},{4,6},{5,7},{6,4},{7,5},{8,10},{9,11},{10,... | collective-permute-start | bytes 786440 | tf_op jit(solution)/shard_map/ppermute | solution.py:76
  38.1 18.9 %collective-permute-start.10 = (bf16[128,1024]{1,0:T(8,128)(2,1)}, bf16[128,1024]{1,0:T(8,128)(2,1)S(1)}, u32[]{:S(2)}, u32[]{:S(2)}) collective-permute-start(bf16[128,1024]{1,0:T(8,128)(2,1)} %get-tuple-element.36), channel_id=1, source_target_pairs={{0,3},{1,0},{2,1},{3,2},{4,7},{5,4},{6,5},{7,6},{8,11},{9,8},{10,9... | collective-permute-start | bytes 786440 | tf_op jit(solution)/shard_map/ppermute | solution.py:76
  40.1 16.9 %collective-permute-start.9 = (bf16[128,1024]{1,0:T(8,128)(2,1)}, bf16[128,1024]{1,0:T(8,128)(2,1)S(1)}, u32[]{:S(2)}, u32[]{:S(2)}) collective-permute-start(bf16[128,1024]{1,0:T(8,128)(2,1)} %get-tuple-element.36), channel_id=1, source_target_pairs={{0,1},{1,2},{2,3},{3,0},{4,5},{5,6},{6,7},{7,4},{8,9},{9,10},{10,1... | collective-permute-start | bytes 786440 | tf_op jit(solution)/shard_map/ppermute | solution.py:76
  56.3 1.9 %collective-permute-start.12 = (f32[8,128]{1,0:T(8,128)}, f32[8,128]{1,0:T(8,128)S(1)}, u32[]{:S(2)}, u32[]{:S(2)}) collective-permute-start(f32[8,128]{1,0:T(8,128)} %get-tuple-element.38.refs_0_), channel_id=1, source_target_pairs={{0,4},{4,0},{1,5},{5,1},{2,6},{6,2},{3,7},{7,3},{8,12},{12,8},{9,1... | collective-permute-start | bytes 12296 | tf_op jit(solution)/shard_map/ppermute | solution.py:26
  57.0 12.8 %copy-start.11 = (bf16[128,1024]{1,0:T(8,128)(2,1)}, bf16[128,1024]{1,0:T(8,128)(2,1)S(1)}, u32[]{:S(2)}) copy-start(bf16[128,1024]{1,0:T(8,128)(2,1)S(1)} %collective-permute-done.11.refs_13_) | copy-start | bytes 786436
  57.0 12.8 %copy-start.12 = (bf16[128,1024]{1,0:T(8,128)(2,1)}, bf16[128,1024]{1,0:T(8,128)(2,1)S(1)}, u32[]{:S(2)}) copy-start(bf16[128,1024]{1,0:T(8,128)(2,1)S(1)} %collective-permute-done.10.refs_12_) | copy-start | bytes 786436
  57.0 12.8 %copy-start.13 = (bf16[128,1024]{1,0:T(8,128)(2,1)}, bf16[128,1024]{1,0:T(8,128)(2,1)S(1)}, u32[]{:S(2)}) copy-start(bf16[128,1024]{1,0:T(8,128)(2,1)S(1)} %collective-permute-done.9.refs_11_) | copy-start | bytes 786436
  57.0 12.8 %collective-permute-start.15 = (bf16[128,1024]{1,0:T(8,128)(2,1)S(1)}, bf16[128,1024]{1,0:T(8,128)(2,1)S(1)}, u32[]{:S(2)}, u32[]{:S(2)}) collective-permute-start(bf16[128,1024]{1,0:T(8,128)(2,1)S(1)} %collective-permute-done.9.refs_11_), channel_id=1, source_target_pairs={{0,4},{4,0},{1,5},{5,1},{2,6},{6,2},{3,7},{7,3},{8,12},{12,8},{9,1... | collective-permute-start | bytes 786440 | tf_op jit(solution)/shard_map/ppermute | solution.py:26
  57.1 12.7 %collective-permute-start.16 = (bf16[128,1024]{1,0:T(8,128)(2,1)S(1)}, bf16[128,1024]{1,0:T(8,128)(2,1)S(1)}, u32[]{:S(2)}, u32[]{:S(2)}) collective-permute-start(bf16[128,1024]{1,0:T(8,128)(2,1)S(1)} %collective-permute-done.10.refs_12_), channel_id=1, source_target_pairs={{0,4},{4,0},{1,5},{5,1},{2,6},{6,2},{3,7},{7,3},{8,12},{12,8},{9,1... | collective-permute-start | bytes 786440 | tf_op jit(solution)/shard_map/ppermute | solution.py:26
  57.6 12.2 %collective-permute-start.17 = (bf16[128,1024]{1,0:T(8,128)(2,1)S(1)}, bf16[128,1024]{1,0:T(8,128)(2,1)S(1)}, u32[]{:S(2)}, u32[]{:S(2)}) collective-permute-start(bf16[128,1024]{1,0:T(8,128)(2,1)S(1)} %collective-permute-done.11.refs_13_), channel_id=1, source_target_pairs={{0,4},{4,0},{1,5},{5,1},{2,6},{6,2},{3,7},{7,3},{8,12},{12,8},{9,1... | collective-permute-start | bytes 786440 | tf_op jit(solution)/shard_map/ppermute | solution.py:26
  57.7 12.1 %collective-permute-start.13 = (bf16[1024,1024]{1,0:T(8,128)(2,1)}, bf16[1024,1024]{1,0:T(8,128)(2,1)S(1)}, u32[]{:S(2)}, u32[]{:S(2)}) collective-permute-start(bf16[1024,1024]{1,0:T(8,128)(2,1)} %get-tuple-element.42), channel_id=1, source_target_pairs={{0,4},{4,0},{1,5},{5,1},{2,6},{6,2},{3,7},{7,3},{8,12},{12,8},{9,1... | collective-permute-start | bytes 6291464 | tf_op jit(solution)/shard_map/ppermute | solution.py:26
  58.1 11.6 %copy-start.17 = (f32[8,128]{1,0:T(8,128)}, f32[8,128]{1,0:T(8,128)S(1)}, u32[]{:S(2)}) copy-start(f32[8,128]{1,0:T(8,128)S(1)} %collective-permute-done.12.refs_1_) | copy-start | bytes 12292
  58.1 11.7 %collective-permute-start.14 = (bf16[1024,1024]{1,0:T(8,128)(2,1)}, bf16[1024,1024]{1,0:T(8,128)(2,1)}, u32[]{:S(2)}, u32[]{:S(2)}) collective-permute-start(bf16[1024,1024]{1,0:T(8,128)(2,1)} %get-tuple-element.44), channel_id=1, source_target_pairs={{0,4},{4,0},{1,5},{5,1},{2,6},{6,2},{3,7},{7,3},{8,12},{12,8},{9,1... | collective-permute-start | bytes 6291464 | tf_op jit(solution)/shard_map/ppermute | solution.py:26
  (12 other events, 42.6 us)
